TPU v7x, 512 devices: a whole 4x4x16 slice. The times are simulated.
512 devices in a mesh: pix: 32 (over z_lo, y), mass: 16 (over z_hi, x, core).
Axes of the slice: x: 4, y: 4, z: 16 (z_hi: 2, z_lo: 8; z = z_hi * 8 + z_lo), core: 2. Of those that a mesh axis runs over, the one named last changes fastest.
Arguments:
- tiles: bfloat16 [32, 16, 16, 256, 256], P('pix', 'mass'), may hold values from 10 to 1000
- tile_pos: int32 [32, 16, 16], P('pix', 'mass'), may hold values from 0 to 255, as said below
- kept_tile_count: int32 [32, 16], P('pix', 'mass'), may hold values from 1 to 16, as said below
- loading: float32 [64, 65536], P('mass', 'pix'), may hold values from 0.006 to 6.5, as said below
- spectra: float32 [64, 131072], P('pix', 'mass'), may hold values from 0.006 to 6.5, as said below
Outputs:
- loading_new: float32 [64, 65536], P('mass', 'pix')
- spectra_new: float32 [64, 131072], P('pix', 'mass')
Inputs may be any that keep to these rules, and one draw needn't show every extreme that they name: `tile_pos`: on each device the 16 entries are distinct; entry q names tile row q // 32 and tile column q % 32 of the device's block. `kept_tile_count`: some device holds exactly 16 kept tiles. `loading`: every entry is positive. `spectra`: every entry is positive.
All inputs are finite; a program needn't handle non-finite values.
Results may differ from a plain program's by a relative error of at most 0.00065.
Values may be sent and summed in bfloat16 or wider, within the bound.
No kernel may reach another device: no remote copies, remote signals or barrier semaphores. Data moves between devices by JAX's collectives and lax.ppermute only.
A program may use at most 64 MiB of HBM per device.

v0:
```python
import jax
import jax.numpy as jnp
from jax import lax
from jax.sharding import PartitionSpec as P


def local(tiles, tile_pos, kept_tile_count, loading, spectra):
    largest_value = lax.Precision.HIGHEST
    stacked_tiles = tiles[0, 0]
    places = tile_pos[0, 0]
    kept_count = kept_tile_count[0, 0]
    slot_count = stacked_tiles.shape[0]
    tile_size = stacked_tiles.shape[1]
    mass_size = lax.axis_size("mass")
    rank_size = loading.shape[0] * mass_size
    pix_dev = loading.shape[1]
    bins_dev = spectra.shape[1]
    tile_rows = pix_dev // tile_size
    tile_cols = bins_dev // tile_size
    live_mask = (jnp.arange(slot_count) < kept_count).astype(jnp.float32)
    row_of = places // tile_cols
    col_of = places % tile_cols
    row_hot = (row_of[:, None] == jnp.arange(tile_rows)[None, :]).astype(jnp.float32) * live_mask[
        :, None
    ]
    column_onehot = (col_of[:, None] == jnp.arange(tile_cols)[None, :]).astype(
        jnp.float32
    ) * live_mask[:, None]
    whole_load = lax.all_gather(loading.astype(jnp.bfloat16), "mass", axis=0, tiled=True)
    gram_load = lax.psum(
        jnp.einsum("kp,jp->kj", whole_load, whole_load, preferred_element_type=jnp.float32), "pix"
    )
    selected_loading = jnp.take(whole_load.reshape(rank_size, tile_rows, tile_size), row_of, axis=1)
    spectra_matrix_product = jnp.einsum(
        "tco,com->ctm", selected_loading, stacked_tiles, preferred_element_type=jnp.float32
    )
    spectra_upper = jnp.einsum(
        "xo,xbm->bom", column_onehot, spectra_matrix_product, precision=largest_value
    ).reshape(rank_size, bins_dev)
    top_rows = lax.psum_scatter(spectra_upper, "pix", scatter_dimension=0, tiled=True)
    old_whole = lax.all_gather(spectra.astype(jnp.bfloat16), "pix", axis=0, tiled=True)
    spec_rows = spectra.shape[0]
    gram_rows = lax.dynamic_slice_in_dim(gram_load, lax.axis_index("pix") * spec_rows, spec_rows, 0)
    bottom_rows = jnp.dot(gram_rows, old_whole.astype(jnp.float32), precision=largest_value)
    spectra_new = spectra * top_rows / bottom_rows
    whole_spec = lax.all_gather(spectra_new.astype(jnp.bfloat16), "pix", axis=0, tiled=True)
    picked_spec = jnp.take(whole_spec.reshape(rank_size, tile_cols, tile_size), col_of, axis=1)
    load_product = jnp.einsum(
        "ksv,suv->sku", picked_spec, stacked_tiles, preferred_element_type=jnp.float32
    )
    load_top = jnp.einsum("sr,sku->kru", row_hot, load_product, precision=largest_value).reshape(
        rank_size, pix_dev
    )
    load_rows = loading.shape[0]
    gram_part = jnp.einsum("km,jm->kj", whole_spec, whole_spec, preferred_element_type=jnp.float32)
    top_mine = lax.psum_scatter(load_top, "mass", scatter_dimension=0, tiled=True)
    gram_spec = lax.psum(gram_part, "mass")
    gram_spec_rows = lax.dynamic_slice_in_dim(
        gram_spec, lax.axis_index("mass") * load_rows, load_rows, 0
    )
    load_bottom = jnp.dot(gram_spec_rows, whole_load.astype(jnp.float32), precision=largest_value)
    loading_new = loading * top_mine / load_bottom
    return (loading_new, spectra_new)


def solution(mesh):
    return jax.shard_map(
        local,
        mesh=mesh,
        in_specs=(
            P("pix", "mass", None, None, None),
            P("pix", "mass", None),
            P("pix", "mass"),
            P("mass", "pix"),
            P("pix", "mass"),
        ),
        out_specs=(P("mass", "pix"), P("pix", "mass")),
        check_vma=False,
    )
```

profile of v0, /device:TPU:1, one launch (start us, length us, event | category | flops | bytes accessed | tf_op | source)
XLA Modules:
  0.0 1191.5 jit_solution(17400756126792257851)
XLA Ops:
  7.2 1.6 convert_bitcast_fusion.1
  8.9 0.0 all-reduce.5.cloned.1.call-start
  9.6 0.8 convert_bitcast_fusion.2
  10.3 51.4 %all-gather = bf16[16,4,2048]{2,1,0:T(4,128)(2,1)S(1)} all-gather(bf16[1,4,2048]{2,1,0:T(4,128)(2,1)S(1)} %convert_bitcast_fusion.2), channel_id=1, replica_groups=mesh['pix'=32,'mass'=16] {'mass'}, dimensions={0}, use_global_device_ids=true | all-gather | bytes 278528 | tf_op jit(solution)/shard_map/all_gather | solution.py:29
  61.7 0.2 reshape.169
  62.0 0.7 fusion.29
  62.6 0.6 gather_fusion
  63.3 0.5 fusion.2
  63.8 2.3 fusion.6
  66.1 2.5 copy.19
  68.7 0.0 all-gather.8.cloned.1.call-start
  68.7 0.1 reshape.190
  68.8 1.3 dynamic-slice
  70.7 0.2 fusion.36
  70.9 203.7 %psum.14 = f32[64,64]{1,0:T(8,128)} all-reduce(f32[64,64]{1,0:T(8,128)S(1)} %fusion.36), channel_id=1, replica_groups=mesh['pix'=32,'mass'=16] {'pix'}, use_global_device_ids=true, to_apply=%region_1.2 | all-reduce | flops 4096 | bytes 32768 | tf_op jit(solution)/shard_map/psum | solution.py:30
  274.7 1.5 reshape.192
  276.1 399.9 %all-reduce.5.cloned.1.call-done = f32[64,8192]{1,0:T(8,128)} async-done(((f32[64,8192]{1,0:T(8,128)}), f32[64,8192]{1,0:T(8,128)}) %all-reduce.5.cloned.1.call-update) | async-done | bytes 2097168
  676.1 1.5 convolution_divide_fusion
  677.6 0.6 convert_bitcast_fusion
  678.3 221.1 %all-gather.8.cloned.1.call-done = bf16[32,2,8192]{2,1,0:T(2,128)(2,1)} async-done(((bf16[1,2,8192]{2,1,0:T(2,128)(2,1)}), bf16[32,2,8192]{2,1,0:T(2,128)(2,1)}) %all-gather.8.cloned.1.call-update) | async-done | bytes 1048592 | tf_op jit(solution)/shard_map/all_gather | solution.py:46
  899.5 1.7 reshape.171
  901.2 1.6 copy.17
  902.8 1.8 gather_fusion.1
  904.6 0.8 fusion
  905.4 1.3 fusion.4
  906.7 1.0 copy.20
  907.6 1.3 dynamic-slice.2
  909.6 1.5 reshape.194
  911.1 0.4 fusion.37
  911.5 131.7 %psum.15 = f32[64,64]{1,0:T(8,128)S(1)} all-reduce(f32[64,64]{1,0:T(8,128)S(1)} %fusion.37), channel_id=1, replica_groups=mesh['pix'=32,'mass'=16] {'mass'}, use_global_device_ids=true, to_apply=%region_3.4 | all-reduce | flops 4096 | bytes 32768 | tf_op jit(solution)/shard_map/psum | solution.py:57
  1043.2 140.1 %all-reduce.7.cloned.1.call-done = f32[64,2048]{1,0:T(8,128)} async-done(((f32[64,2048]{1,0:T(8,128)}), f32[64,2048]{1,0:T(8,128)}) %all-reduce.7.cloned.1.call-update) | async-done | bytes 524304
  1183.3 1.7 convolution_divide_fusion.1
  (21 shorter events, 0.3 us)
Async XLA Ops:
  7.2 56.1 %copy-start = (bf16[1,1,16,256,256]{4,3,2,1,0:T(8,128)(2,1)S(1)}, bf16[1,1,16,256,256]{4,3,2,1,0:T(8,128)(2,1)}, u32[]{:S(2)}) copy-start(bf16[1,1,16,256,256]{4,3,2,1,0:T(8,128)(2,1)} %param.5) | copy-start | bytes 6291460
  7.2 56.0 %copy-start.4 = (s32[1,1,16]{2,1,0:T(1,128)S(1)}, s32[1,1,16]{2,1,0:T(1,128)}, u32[]{:S(2)}) copy-start(s32[1,1,16]{2,1,0:T(1,128)} %param.6) | copy-start | bytes 196
  7.2 267.5 %all-gather.6.cloned.1.call-start = ((), (), s32[]{:S(2)}) async-start(), calls=%async_computation | async-start | bytes 1081344 | tf_op jit(solution)/shard_map/all_gather | solution.py:41
  8.9 667.2 %all-reduce.5.cloned.1.call-start = ((), (), s32[]{:S(2)}) async-start(), calls=%async_computation.2 | async-start | bytes 4194304
  68.7 607.4 %copy-start.1 = (f32[2,8192]{1,0:T(2,128)S(1)}, f32[2,8192]{1,0:T(2,128)}, u32[]{:S(2)}) copy-start(f32[2,8192]{1,0:T(2,128)} %param.9) | copy-start | bytes 196612
  68.7 830.8 %all-gather.8.cloned.1.call-start = ((), (), s32[]{:S(2)}) async-start(), calls=%async_computation.1 | async-start | bytes 1081344 | tf_op jit(solution)/shard_map/all_gather | solution.py:46
  677.6 225.2 %copy-start.2 = (f32[2,8192]{1,0:T(2,128)}, f32[2,8192]{1,0:T(2,128)S(1)}, u32[]{:S(2)}) copy-start(f32[2,8192]{1,0:T(2,128)S(1)} %convolution_divide_fusion) | copy-start | bytes 196612
  678.3 505.0 %all-reduce.7.cloned.1.call-start = ((), (), s32[]{:S(2)}) async-start(), calls=%async_computation.3 | async-start | bytes 1048576
  909.6 273.7 %copy-start.3 = (f32[4,2048]{1,0:T(4,128)S(1)}, f32[4,2048]{1,0:T(4,128)}, u32[]{:S(2)}) copy-start(f32[4,2048]{1,0:T(4,128)} %param.8) | copy-start | bytes 98308
Sparse Core Ops, SparseCore 0:
  10.7 205.9 all-gather.5
  219.6 456.4 all-reduce.4
  678.9 220.4 all-gather.7
  907.8 275.4 all-reduce.6
where the time goes:
time: 1190 us
  waiting for transfers between devices  761 us (64%)
  blocking collectives  387 us (33%)
  between operations  15.9 us (1%)
  local copies, waits for them, and re-layouts  15 us (1%)
    unnamed x6, waiting for transfers between devices  540 us
    all_gather x1, waiting for transfers between devices, local(): lax.all_gather(spectra_new.astype(jnp.bfloat16), 'pix', axis=0, tiled=True)  221 us
    psum x1, blocking collectives, local(): lax.psum(jnp.einsum('kp,jp->kj', whole_load, whole_load, preferred_elemen...  204 us
    psum x1, blocking collectives, local(): gram_spec = lax.psum(gram_part, 'mass')  132 us
    all_gather x1, blocking collectives, local(): lax.all_gather(loading.astype(jnp.bfloat16), 'mass', axis=0, tiled=True)  51.4 us
  transfers between devices with their start and end apart: 4, of which 3 were waited for; matrix products, arithmetic and copies ran while one was open for 1% of the time, Pallas kernels for 0%

commit v1 on v0

v1 whole, which is shorter than its diff:
```python
import jax
import jax.numpy as jnp
from jax import lax
from jax.experimental import pallas as pl
from jax.experimental.pallas import tpu as pltpu
from jax.sharding import Mesh, PartitionSpec as P

F32, BF16, F16 = jnp.float32, jnp.bfloat16, jnp.float16
PIX = ("zl", "y")
MASS = ("zh", "x", "core")
RANK, TILE, TROWS, TCOLS, CAP = 64, 256, 8, 32, 16
NZ, NY, NMASS = 8, 4, 16
PER = RANK // NMASS
TOP_SCALE = 2.0**-10
GRAM_SCALE = 2.0**-3
TOPS = NZ * RANK
PIXELS = TROWS * TILE
WIDE = PIXELS + 128
VMEM = pl.BlockSpec(memory_space=pltpu.VMEM)
SMEM = pl.BlockSpec(memory_space=pltpu.SMEM)
CONTRACT_LAST = (((1,), (1,)), ((), ()))


def spec_kernel(pos_ref, count_ref, load_ref, tiles_ref, spec_ref, out_ref, wide_ref, half_ref):
    for m in range(NMASS):
        wide_ref[pl.ds(PER * m, PER), :] = load_ref[m].astype(F32)
    half_ref[...] = wide_ref[...].astype(BF16)
    for y in range(NY):
        out_ref[y, pl.ds(0, TOPS), :] = jnp.zeros((TOPS, TILE), F32)
    count = count_ref[0]
    for s in range(CAP):
        place = pos_ref[s]
        row, col = place // TCOLS, place % TCOLS
        lanes = pl.ds(pl.multiple_of(row * TILE, TILE), TILE)
        product = jnp.dot(half_ref[:, lanes], tiles_ref[s], preferred_element_type=F32) * TOP_SCALE
        rows = pl.ds(pl.multiple_of((col // NY) * RANK, RANK), RANK)
        out_ref[col % NY, rows, :] += jnp.where(s < count, product, 0.0)
    half = half_ref[...]
    gram = lax.dot_general(half, half, CONTRACT_LAST, preferred_element_type=F32) * GRAM_SCALE
    packed = jnp.concatenate([gram[16 * i : 16 * i + 16, :] for i in range(4)], axis=1)
    for y in range(NY):
        for z in range(NZ):
            c = z * NY + y
            out_ref[y, pl.ds(TOPS + 2 * z, 2), :] = spec_ref[:, c * TILE : (c + 1) * TILE]
        out_ref[y, pl.ds(TOPS + 2 * NZ, 16), :] = packed


def update_kernel(sums_ref, spec_ref, out_ref):
    packed = sums_ref[pl.ds(RANK, 16), :] * (TOP_SCALE / GRAM_SCALE)
    gram = jnp.concatenate([packed[:, RANK * i : RANK * i + RANK] for i in range(4)], axis=0)
    spec = spec_ref[...]
    bottom = jnp.dot(gram, spec.astype(BF16).astype(F32), precision=lax.Precision.HIGHEST, preferred_element_type=F32)
    new = spec * sums_ref[pl.ds(0, RANK), :] / bottom
    fresh = new.astype(BF16)
    rest = new - fresh.astype(F32)
    for z in range(NZ):
        out_ref[z, pl.ds(0, RANK), :] = fresh
        out_ref[z, pl.ds(RANK, 8), :] = rest[8 * z : 8 * z + 8, :].astype(BF16)


def spread_kernel(in_ref, out_ref):
    for y in range(NY):
        for z in range(NZ):
            out_ref[y, pl.ds(z * RANK, RANK), :] = in_ref[z, pl.ds(0, RANK), :]
    for z in range(NZ):
        rest = in_ref[z, pl.ds(RANK, 8), :].astype(F32)
        for y in range(NY):
            out_ref[y, pl.ds(TOPS + 2 * z, 2), :] = rest[2 * y : 2 * y + 2, :].astype(BF16)


def load_kernel(pos_ref, count_ref, fresh_ref, tiles_ref, out_ref, acc_ref):
    acc_ref[...] = jnp.zeros_like(acc_ref)
    count = count_ref[0]
    for s in range(CAP):
        place = pos_ref[s]
        row, col = place // TCOLS, place % TCOLS
        rows = pl.ds(pl.multiple_of((col // NY) * RANK, RANK), RANK)
        block = fresh_ref[col % NY, rows, :]
        product = lax.dot_general(block, tiles_ref[s], CONTRACT_LAST, preferred_element_type=F32)
        lanes = pl.ds(pl.multiple_of(row * TILE, TILE), TILE)
        acc_ref[:, lanes] += jnp.where(s < count, product, 0.0)
    gram = jnp.zeros((RANK, RANK), F32)
    for y in range(NY):
        for z in range(NZ):
            block = fresh_ref[y, pl.ds(z * RANK, RANK), :]
            gram = gram + lax.dot_general(block, block, CONTRACT_LAST, preferred_element_type=F32)

    def exponent(x):
        return jnp.floor(jnp.log2(jnp.maximum(jnp.max(x, axis=1, keepdims=True), 1e-30))) - 13.0

    top = acc_ref[...]
    top_exp, gram_exp = exponent(top), exponent(gram)
    top = top * jnp.exp2(-top_exp)
    gram = gram * jnp.exp2(-gram_exp)
    lane = lax.broadcasted_iota(jnp.int32, (RANK, RANK), 1)
    tail = jnp.where(lane == 0, top_exp, jnp.where(lane == 1, gram_exp, 0.0))
    tail = jnp.concatenate([gram, tail], axis=1)
    for m in range(NMASS):
        out_ref[m, :, pl.ds(0, PIXELS)] = top[PER * m : PER * m + PER, :]
        out_ref[m, :, pl.ds(PIXELS, 128)] = tail[PER * m : PER * m + PER, :]


def spectra_kernel(place_ref, recv_ref, spec_ref, sent_ref, out_ref):
    zl, yl = place_ref[0], place_ref[1]
    for z in range(NZ):
        for y in range(NY):
            c = z * NY + y
            eight = recv_ref[y, pl.ds(pl.multiple_of(z * RANK + 8 * zl, 8), 8), :].astype(F32)
            two = eight[0:2, :]
            for k in range(1, NY):
                two = jnp.where(yl == k, eight[2 * k : 2 * k + 2, :], two)
            rest = recv_ref[y, pl.ds(TOPS + 2 * z, 2), :].astype(F32)
            cols = pl.ds(c * TILE, TILE)
            out_ref[:, cols] = (two + rest) * (spec_ref[:, cols] / sent_ref[:, cols])


def local(tiles, tile_pos, kept_tile_count, loading, spectra):
    tiles = tiles[0, 0]
    pos = tile_pos[0, 0]
    count = kept_tile_count[0]

    own = jnp.broadcast_to(loading.astype(BF16)[None], (NMASS, PER, PIXELS))
    load = lax.all_to_all(own, MASS, 0, 0, tiled=True)
    sent = lax.reduce_precision(spectra, 5, 10)

    out = pl.pallas_call(
        spec_kernel,
        out_shape=jax.ShapeDtypeStruct((NY, TOPS + 32, TILE), F32),
        in_specs=[SMEM, SMEM, VMEM, VMEM, VMEM],
        out_specs=VMEM,
        scratch_shapes=[pltpu.VMEM((RANK, PIXELS), F32), pltpu.VMEM((RANK, PIXELS), BF16)],
        name="spec",
    )(pos, count, load, tiles, sent)
    part = lax.all_to_all(out.astype(F16), "y", 0, 0, tiled=True)
    tops = part[:, :TOPS].astype(F32).sum(0).astype(F16).reshape(NZ, RANK, TILE)
    old = part[:, TOPS : TOPS + 2 * NZ].reshape(NY, NZ, 2, TILE).transpose(1, 0, 2, 3).reshape(NZ, 8, TILE)
    gram = part[:, TOPS + 2 * NZ :].astype(F32).sum(0).astype(F16)
    gram = jnp.broadcast_to(gram[None], (NZ, 16, TILE))
    part = lax.all_to_all(jnp.concatenate([tops, old, gram], axis=1), "zl", 0, 0, tiled=True)
    wide = part.astype(F32)
    sums = jnp.concatenate([wide[:, :RANK].sum(0), wide[:, RANK + 8 :].sum(0)], axis=0)
    old = wide[:, RANK : RANK + 8].reshape(RANK, TILE)

    fresh = pl.pallas_call(
        update_kernel,
        out_shape=jax.ShapeDtypeStruct((NZ, RANK + 8, TILE), BF16),
        in_specs=[VMEM, VMEM],
        out_specs=VMEM,
        name="update",
    )(sums, old)
    fresh = lax.all_to_all(fresh, "zl", 0, 0, tiled=True)
    fresh = pl.pallas_call(
        spread_kernel,
        out_shape=jax.ShapeDtypeStruct((NY, TOPS + 16, TILE), BF16),
        in_specs=[VMEM],
        out_specs=VMEM,
        name="spread",
    )(fresh)
    fresh = lax.all_to_all(fresh, "y", 0, 0, tiled=True)

    out = pl.pallas_call(
        load_kernel,
        out_shape=jax.ShapeDtypeStruct((NMASS, PER, WIDE), F32),
        in_specs=[SMEM, SMEM, VMEM, VMEM],
        out_specs=VMEM,
        scratch_shapes=[pltpu.VMEM((RANK, PIXELS), F32)],
        name="load",
    )(pos, count, fresh, tiles)
    part = lax.all_to_all(out.astype(F16), MASS, 0, 0, tiled=True).astype(F32)

    place = jnp.stack([lax.axis_index("zl"), lax.axis_index("y")]).astype(jnp.int32)
    spectra_new = pl.pallas_call(
        spectra_kernel,
        out_shape=jax.ShapeDtypeStruct(spectra.shape, F32),
        in_specs=[SMEM, VMEM, VMEM, VMEM],
        out_specs=VMEM,
        name="spectra",
    )(place, fresh, spectra, sent)

    exps = part[:, :, PIXELS + RANK : PIXELS + RANK + 2]
    top = (part[:, :, :PIXELS] * jnp.exp2(exps[:, :, 0:1])).sum(0)
    gram = (part[:, :, PIXELS : PIXELS + RANK] * jnp.exp2(exps[:, :, 1:2])).sum(0)
    bottom = jnp.dot(gram, load.reshape(RANK, PIXELS).astype(F32), precision=lax.Precision.HIGHEST)
    loading_new = loading * top / bottom
    return (loading_new, spectra_new)


def solution(mesh):
    fine = Mesh(mesh.devices.reshape(NZ, NY, 2, 4, 2), PIX + MASS)
    return jax.shard_map(
        local,
        mesh=fine,
        in_specs=(P(PIX, MASS, None, None, None), P(PIX, MASS, None), P(PIX, MASS), P(MASS, PIX), P(PIX, MASS)),
        out_specs=(P(MASS, PIX), P(PIX, MASS)),
        check_vma=False,
    )
```

time: 1190 us -> 179 us (0.15)
  the two profiles are of different devices: /device:TPU:1 before, /device:TPU:32 now
where the time goes in v1:
time: 179 us; the launch traced here: 178 us
  blocking collectives  85.7 us (48%)
  waiting for transfers between devices  44.5 us (25%)
  starting transfers between devices  20.7 us (12%)
  Pallas kernels  13.7 us (8%)
  other arithmetic  8.1 us (5%)
  local copies, waits for them, and re-layouts  2.66 us (1%)
    all_to_all x1, blocking collectives, local(): lax.all_to_all(jnp.concatenate([tops, old, gram], axis=1), 'zl', 0, 0, ti...  24.1 us
    all_to_all x1, blocking collectives, local(): fresh = lax.all_to_all(fresh, 'zl', 0, 0, tiled=True)  23.2 us
    all_to_all x1, waiting for transfers between devices, local(): load = lax.all_to_all(own, MASS, 0, 0, tiled=True)  23 us
    all_to_all x1, waiting for transfers between devices, local(): part = lax.all_to_all(out.astype(F16), MASS, 0, 0, tiled=True).astype(F32)  21.6 us
    all_to_all x1, blocking collectives, local(): part = lax.all_to_all(out.astype(F16), 'y', 0, 0, tiled=True)  19.8 us
    all_to_all x1, blocking collectives, local(): fresh = lax.all_to_all(fresh, 'y', 0, 0, tiled=True)  18.7 us
    all_to_all x1, starting transfers between devices, local(): load = lax.all_to_all(own, MASS, 0, 0, tiled=True)  16.8 us
    pallas_call x1, Pallas kernels, local(): pl.pallas_call(load_kernel, out_shape=jax.ShapeDtypeStruct((NMASS, PER, W...  3.96 us
  transfers between devices with their start and end apart: 2, of which 2 were waited for; matrix products, arithmetic and copies ran while one was open for 1% of the time, Pallas kernels for 1%

profile of v1, /device:TPU:32, one launch (start us, length us, event | category | flops | bytes accessed | tf_op | source)
XLA Modules:
  0.0 177.7 jit_solution(17733205374270803589)
XLA Ops:
  0.6 0.8 convert_element_type.36
  1.4 0.8 broadcast_in_dim.4
  2.2 16.8 %all-to-all-start = ((bf16[16,4,2048]{2,1,0:T(4,128)(2,1)}), bf16[16,4,2048]{2,1,0:T(4,128)(2,1)S(1)}, u32[]{:S(2)}, u32[]{:S(2)}) async-start(bf16[16,4,2048]{2,1,0:T(4,128)(2,1)} %broadcast_in_dim.4), calls=%async_computation | async-start | bytes 524288 | tf_op jit(solution)/shard_map/all_to_all | solution.py:123
  19.0 1.6 reduce_precision.3.spec_ref.sent_ref
  21.2 23.0 %all-to-all-done.load_ref = bf16[16,4,2048]{2,1,0:T(4,128)(2,1)S(1)} async-done(((bf16[16,4,2048]{2,1,0:T(4,128)(2,1)}), bf16[16,4,2048]{2,1,0:T(4,128)(2,1)S(1)}, u32[]{:S(2)}, u32[]{:S(2)}) %all-to-all-start) | async-done | bytes 262176 | tf_op jit(solution)/shard_map/all_to_all | solution.py:123
  44.1 0.7 copy-done
  44.8 3.8 %spec.1 = f32[4,544,256]{2,1,0:T(8,128)} custom-call(s32[16]{0:T(128)} %bitcast.21, s32[1]{0:T(128)} %bitcast.13.count_ref, bf16[16,4,2048]{2,1,0:T(4,128)(2,1)} %copy-done, bf16[16,256,256]{2,1,0:T(8,128)(2,1)} %bitcast.15, f32[2,8192]{1,0:T(2,128)} %reduce_precision.3.spec_ref.sent_ref), custom_call_target="tpu_custom_call" | custom-call | tf_op jit(solution)/shard_map/spec/pallas_call | solution.py:126
  48.6 1.8 %convert_element_type.37 = f16[4,544,256]{2,1,0:T(8,128)(2,1)S(1)} convert(f32[4,544,256]{2,1,0:T(8,128)} %spec.1) | non-fusion elementwise | flops 557056 | bytes 3342336 | tf_op jit(solution)/shard_map/convert_element_type | solution.py:134
  50.4 19.8 %all_to_all.30 = f16[4,544,256]{2,1,0:T(8,128)(2,1)S(1)} all-to-all(f16[4,544,256]{2,1,0:T(8,128)(2,1)S(1)} %convert_element_type.37), channel_id=1, replica_groups=mesh['zl'=8,'y'=4,'zh'=2,'x'=4,'core'=2] {'y'}, dimensions={0} | all-to-all | bytes 2228224 | tf_op jit(solution)/shard_map/all_to_all | solution.py:134
  70.2 0.1 convert_reduce_fusion
  70.5 0.1 pad_maximum_fusion
  70.6 24.1 %all_to_all.31 = f16[8,88,256]{2,1,0:T(8,128)(2,1)S(1)} all-to-all(f16[8,88,256]{2,1,0:T(8,128)(2,1)S(1)} %pad_maximum_fusion), channel_id=1, replica_groups=mesh['zl'=8,'y'=4,'zh'=2,'x'=4,'core'=2] {'zl'}, dimensions={0} | all-to-all | bytes 720896 | tf_op jit(solution)/shard_map/all_to_all | solution.py:139
  94.8 0.6 slice_bitcast_fusion.spec_ref
  95.5 0.6 pad_maximum_fusion.1.sums_ref
  96.1 1.9 %update.1 = bf16[8,72,256]{2,1,0:T(8,128)(2,1)} custom-call(f32[80,256]{1,0:T(8,128)} %pad_maximum_fusion.1.sums_ref, f32[64,256]{1,0:T(8,128)} %slice_bitcast_fusion.spec_ref), custom_call_target="tpu_custom_call" | custom-call | tf_op jit(solution)/shard_map/update/pallas_call | solution.py:144
  98.0 23.2 %all_to_all.32.in_ref = bf16[8,72,256]{2,1,0:T(8,128)(2,1)} all-to-all(bf16[8,72,256]{2,1,0:T(8,128)(2,1)} %update.1), channel_id=1, replica_groups=mesh['zl'=8,'y'=4,'zh'=2,'x'=4,'core'=2] {'zl'}, dimensions={0} | all-to-all | bytes 589824 | tf_op jit(solution)/shard_map/all_to_all | solution.py:151
  121.1 2.1 %spread.1 = bf16[4,528,256]{2,1,0:T(8,128)(2,1)} custom-call(bf16[8,72,256]{2,1,0:T(8,128)(2,1)} %all_to_all.32.in_ref), custom_call_target="tpu_custom_call" | custom-call | tf_op jit(solution)/shard_map/spread/pallas_call | solution.py:152
  123.2 18.7 %all_to_all.33.fresh_ref.recv_ref = bf16[4,528,256]{2,1,0:T(8,128)(2,1)} all-to-all(bf16[4,528,256]{2,1,0:T(8,128)(2,1)} %spread.1), channel_id=1, replica_groups=mesh['zl'=8,'y'=4,'zh'=2,'x'=4,'core'=2] {'y'}, dimensions={0} | all-to-all | bytes 2162688 | tf_op jit(solution)/shard_map/all_to_all | solution.py:159
  141.9 4.0 %load.1 = f32[16,4,2176]{2,1,0:T(4,128)} custom-call(s32[16]{0:T(128)} %bitcast.22, s32[1]{0:T(128)} %bitcast.14.count_ref, bf16[4,528,256]{2,1,0:T(8,128)(2,1)} %all_to_all.33.fresh_ref.recv_ref, bf16[16,256,256]{2,1,0:T(8,128)(2,1)} %bitcast.16), custom_call_target="tpu_custom_call" | custom-call | tf_op jit(solution)/shard_map/load/pallas_call | solution.py:161
  145.9 1.9 %convert_element_type.44 = f16[16,4,2176]{2,1,0:T(4,128)(2,1)} convert(f32[16,4,2176]{2,1,0:T(4,128)} %load.1) | non-fusion elementwise | flops 139264 | bytes 835584 | tf_op jit(solution)/shard_map/convert_element_type | solution.py:169
  147.8 4.0 %all-to-all-start.5 = ((f16[16,4,2176]{2,1,0:T(4,128)(2,1)}), f16[16,4,2176]{2,1,0:T(4,128)(2,1)S(1)}, u32[]{:S(2)}, u32[]{:S(2)}) async-start(f16[16,4,2176]{2,1,0:T(4,128)(2,1)} %convert_element_type.44), calls=%async_computation.5 | async-start | bytes 557056 | tf_op jit(solution)/shard_map/all_to_all | solution.py:169
  151.7 0.6 pad_add_fusion.place_ref
  152.4 2.1 %spectra.1 = f32[2,8192]{1,0:T(2,128)} custom-call(s32[2]{0:T(128)} %pad_add_fusion.place_ref, bf16[4,528,256]{2,1,0:T(8,128)(2,1)} %all_to_all.33.fresh_ref.recv_ref, f32[2,8192]{1,0:T(2,128)} %spec_ref.1, f32[2,8192]{1,0:T(2,128)} %reduce_precision.3.spec_ref.sent_ref), custom_call_target="tpu_custom_call" | custom-call | tf_op jit(solution)/shard_map/spectra/pallas_call | solution.py:172
  154.4 21.6 %all-to-all-done.5 = f16[16,4,2176]{2,1,0:T(4,128)(2,1)S(1)} async-done(((f16[16,4,2176]{2,1,0:T(4,128)(2,1)}), f16[16,4,2176]{2,1,0:T(4,128)(2,1)S(1)}, u32[]{:S(2)}, u32[]{:S(2)}) %all-to-all-start.5) | async-done | bytes 278560 | tf_op jit(solution)/shard_map/all_to_all | solution.py:169
  176.0 0.1 convert_element_type.45
  176.1 0.1 fusion.3
  176.2 0.1 copy.14
  176.3 0.1 copy.15
  176.4 0.2 fusion
  176.6 0.1 copy.17
  176.8 0.1 fusion.2
  176.9 0.8 convolution_divide_fusion
  (18 shorter events, 0.4 us)
Async XLA Ops:
  2.2 42.0 %all-to-all-start = ((bf16[16,4,2048]{2,1,0:T(4,128)(2,1)}), bf16[16,4,2048]{2,1,0:T(4,128)(2,1)S(1)}, u32[]{:S(2)}, u32[]{:S(2)}) async-start(bf16[16,4,2048]{2,1,0:T(4,128)(2,1)} %broadcast_in_dim.4), calls=%async_computation | async-start | bytes 524288 | tf_op jit(solution)/shard_map/all_to_all | solution.py:123
  44.1 0.7 copy-start
  145.9 6.4 %copy-start.1 = (bf16[16,4,2048]{2,1,0:T(4,128)(2,1)S(1)}, bf16[16,4,2048]{2,1,0:T(4,128)(2,1)}, u32[]{:S(2)}) copy-start(bf16[16,4,2048]{2,1,0:T(4,128)(2,1)} %copy-done) | copy-start | bytes 786436
  147.8 28.2 %all-to-all-start.5 = ((f16[16,4,2176]{2,1,0:T(4,128)(2,1)}), f16[16,4,2176]{2,1,0:T(4,128)(2,1)S(1)}, u32[]{:S(2)}, u32[]{:S(2)}) async-start(f16[16,4,2176]{2,1,0:T(4,128)(2,1)} %convert_element_type.44), calls=%async_computation.5 | async-start | bytes 557056 | tf_op jit(solution)/shard_map/all_to_all | solution.py:169
  154.4 22.5 %copy-start.2 = (f32[4,2048]{1,0:T(4,128)S(1)}, f32[4,2048]{1,0:T(4,128)}, u32[]{:S(2)}) copy-start(f32[4,2048]{1,0:T(4,128)} %param.8) | copy-start | bytes 98308

commit v2 on v1

--- a/solution.py
+++ b/solution.py
@@ -18,6 +18,7 @@
 WIDE = PIXELS + 128
 VMEM = pl.BlockSpec(memory_space=pltpu.VMEM)
 SMEM = pl.BlockSpec(memory_space=pltpu.SMEM)
+PARAMS = pltpu.CompilerParams(vmem_limit_bytes=12 << 20)
 CONTRACT_LAST = (((1,), (1,)), ((), ()))
 
 
@@ -114,6 +115,10 @@
             out_ref[:, cols] = (two + rest) * (spec_ref[:, cols] / sent_ref[:, cols])
 
 
+def near(x):
+    return pltpu.with_memory_space_constraint(x, pltpu.VMEM)
+
+
 def local(tiles, tile_pos, kept_tile_count, loading, spectra):
     tiles = tiles[0, 0]
     pos = tile_pos[0, 0]
@@ -125,12 +130,13 @@
 
     out = pl.pallas_call(
         spec_kernel,
-        out_shape=jax.ShapeDtypeStruct((NY, TOPS + 32, TILE), F32),
+        out_shape=pltpu.VMEM((NY, TOPS + 32, TILE), F32),
         in_specs=[SMEM, SMEM, VMEM, VMEM, VMEM],
         out_specs=VMEM,
         scratch_shapes=[pltpu.VMEM((RANK, PIXELS), F32), pltpu.VMEM((RANK, PIXELS), BF16)],
+        compiler_params=PARAMS,
         name="spec",
-    )(pos, count, load, tiles, sent)
+    )(pos, count, near(load), near(tiles), near(sent))
     part = lax.all_to_all(out.astype(F16), "y", 0, 0, tiled=True)
     tops = part[:, :TOPS].astype(F32).sum(0).astype(F16).reshape(NZ, RANK, TILE)
     old = part[:, TOPS : TOPS + 2 * NZ].reshape(NY, NZ, 2, TILE).transpose(1, 0, 2, 3).reshape(NZ, 8, TILE)
@@ -143,29 +149,32 @@
 
     fresh = pl.pallas_call(
         update_kernel,
-        out_shape=jax.ShapeDtypeStruct((NZ, RANK + 8, TILE), BF16),
+        out_shape=pltpu.VMEM((NZ, RANK + 8, TILE), BF16),
         in_specs=[VMEM, VMEM],
         out_specs=VMEM,
+        compiler_params=PARAMS,
         name="update",
-    )(sums, old)
+    )(near(sums), near(old))
     fresh = lax.all_to_all(fresh, "zl", 0, 0, tiled=True)
     fresh = pl.pallas_call(
         spread_kernel,
-        out_shape=jax.ShapeDtypeStruct((NY, TOPS + 16, TILE), BF16),
+        out_shape=pltpu.VMEM((NY, TOPS + 16, TILE), BF16),
         in_specs=[VMEM],
         out_specs=VMEM,
+        compiler_params=PARAMS,
         name="spread",
-    )(fresh)
+    )(near(fresh))
     fresh = lax.all_to_all(fresh, "y", 0, 0, tiled=True)
 
     out = pl.pallas_call(
         load_kernel,
-        out_shape=jax.ShapeDtypeStruct((NMASS, PER, WIDE), F32),
+        out_shape=pltpu.VMEM((NMASS, PER, WIDE), F32),
         in_specs=[SMEM, SMEM, VMEM, VMEM],
         out_specs=VMEM,
         scratch_shapes=[pltpu.VMEM((RANK, PIXELS), F32)],
+        compiler_params=PARAMS,
         name="load",
-    )(pos, count, fresh, tiles)
+    )(pos, count, near(fresh), near(tiles))
     part = lax.all_to_all(out.astype(F16), MASS, 0, 0, tiled=True).astype(F32)
 
     place = jnp.stack([lax.axis_index("zl"), lax.axis_index("y")]).astype(jnp.int32)
@@ -174,8 +183,9 @@
         out_shape=jax.ShapeDtypeStruct(spectra.shape, F32),
         in_specs=[SMEM, VMEM, VMEM, VMEM],
         out_specs=VMEM,
+        compiler_params=PARAMS,
         name="spectra",
-    )(place, fresh, spectra, sent)
+    )(place, near(fresh), near(spectra), near(sent))
 
     exps = part[:, :, PIXELS + RANK : PIXELS + RANK + 2]
     top = (part[:, :, :PIXELS] * jnp.exp2(exps[:, :, 0:1])).sum(0)

time: 179 us -> 166 us (0.927)
  Pallas kernels: 13.7 us -> 4.76 us
  other arithmetic: 8.1 us -> 3.69 us
  blocking collectives: 85.7 us -> 83.6 us
  waiting for transfers between devices: 44.5 us -> 46.4 us
    pallas_call x4, Pallas kernels: 11.7 us -> 3.46 us  [the longest x1 1.77 us: local(): pl.pallas_call(load_kernel, out_shape=pltpu.VMEM((NMASS, PER, WIDE), F32)...]
where the time goes in v2:
time: 166 us; the launch traced here: 165 us
  blocking collectives  83.6 us (50%)
  waiting for transfers between devices  46.4 us (28%)
  starting transfers between devices  20.7 us (12%)
  Pallas kernels  4.76 us (3%)
  other arithmetic  3.69 us (2%)
  local copies, waits for them, and re-layouts  3.6 us (2%)
    all_to_all x1, blocking collectives, local(): lax.all_to_all(jnp.concatenate([tops, old, gram], axis=1), 'zl', 0, 0, ti...  24.1 us
    all_to_all x1, waiting for transfers between devices, local(): load = lax.all_to_all(own, MASS, 0, 0, tiled=True)  23.6 us
    all_to_all x1, blocking collectives, local(): fresh = lax.all_to_all(fresh, 'zl', 0, 0, tiled=True)  22.9 us
    all_to_all x1, waiting for transfers between devices, local(): part = lax.all_to_all(out.astype(F16), MASS, 0, 0, tiled=True).astype(F32)  22.8 us
    all_to_all x1, blocking collectives, local(): part = lax.all_to_all(out.astype(F16), 'y', 0, 0, tiled=True)  19.8 us
    all_to_all x1, blocking collectives, local(): fresh = lax.all_to_all(fresh, 'y', 0, 0, tiled=True)  16.9 us
    all_to_all x1, starting transfers between devices, local(): load = lax.all_to_all(own, MASS, 0, 0, tiled=True)  16.8 us
    all_to_all x1, starting transfers between devices, local(): part = lax.all_to_all(out.astype(F16), MASS, 0, 0, tiled=True).astype(F32)  3.93 us
  transfers between devices with their start and end apart: 2, of which 2 were waited for; matrix products, arithmetic and copies ran while one was open for 1% of the time, Pallas kernels for 1%

profile of v2, /device:TPU:32, one launch (start us, length us, event | category | flops | bytes accessed | tf_op | source)
XLA Modules:
  0.0 165.1 jit_solution(136363201078161992)
XLA Ops:
  0.6 0.8 convert_element_type.36
  1.4 0.8 broadcast_in_dim.4
  2.2 16.8 %all-to-all-start = ((bf16[16,4,2048]{2,1,0:T(4,128)(2,1)}), bf16[16,4,2048]{2,1,0:T(4,128)(2,1)S(1)}, u32[]{:S(2)}, u32[]{:S(2)}) async-start(bf16[16,4,2048]{2,1,0:T(4,128)(2,1)} %broadcast_in_dim.4), calls=%async_computation | async-start | bytes 524288 | tf_op jit(solution)/shard_map/all_to_all | solution.py:128
  19.0 1.0 reduce_precision.3.spec_ref.sent_ref
  20.6 23.6 %all-to-all-done.load_ref = bf16[16,4,2048]{2,1,0:T(4,128)(2,1)S(1)} async-done(((bf16[16,4,2048]{2,1,0:T(4,128)(2,1)}), bf16[16,4,2048]{2,1,0:T(4,128)(2,1)S(1)}, u32[]{:S(2)}, u32[]{:S(2)}) %all-to-all-start) | async-done | bytes 262176 | tf_op jit(solution)/shard_map/all_to_all | solution.py:128
  44.1 1.6 copy-done
  45.7 0.7 copy-done.3
  46.4 1.3 spec.1
  47.7 0.2 convert_element_type.37
  48.0 19.8 %all_to_all.30 = f16[4,544,256]{2,1,0:T(8,128)(2,1)S(1)} all-to-all(f16[4,544,256]{2,1,0:T(8,128)(2,1)S(1)} %convert_element_type.37), channel_id=1, replica_groups=mesh['zl'=8,'y'=4,'zh'=2,'x'=4,'core'=2] {'y'}, dimensions={0} | all-to-all | bytes 2228224 | tf_op jit(solution)/shard_map/all_to_all | solution.py:140
  67.7 0.1 convert_reduce_fusion
  68.1 0.1 pad_maximum_fusion
  68.2 24.1 %all_to_all.31 = f16[8,88,256]{2,1,0:T(8,128)(2,1)S(1)} all-to-all(f16[8,88,256]{2,1,0:T(8,128)(2,1)S(1)} %pad_maximum_fusion), channel_id=1, replica_groups=mesh['zl'=8,'y'=4,'zh'=2,'x'=4,'core'=2] {'zl'}, dimensions={0} | all-to-all | bytes 720896 | tf_op jit(solution)/shard_map/all_to_all | solution.py:145
  92.4 0.3 update.1
  92.7 22.9 %all_to_all.32.in_ref = bf16[8,72,256]{2,1,0:T(8,128)(2,1)S(1)} all-to-all(bf16[8,72,256]{2,1,0:T(8,128)(2,1)S(1)} %update.1), channel_id=1, replica_groups=mesh['zl'=8,'y'=4,'zh'=2,'x'=4,'core'=2] {'zl'}, dimensions={0} | all-to-all | bytes 589824 | tf_op jit(solution)/shard_map/all_to_all | solution.py:158
  115.6 0.1 spread.1
  115.7 16.9 %all_to_all.33.fresh_ref.recv_ref = bf16[4,528,256]{2,1,0:T(8,128)(2,1)S(1)} all-to-all(bf16[4,528,256]{2,1,0:T(8,128)(2,1)S(1)} %spread.1), channel_id=1, replica_groups=mesh['zl'=8,'y'=4,'zh'=2,'x'=4,'core'=2] {'y'}, dimensions={0} | all-to-all | bytes 2162688 | tf_op jit(solution)/shard_map/all_to_all | solution.py:167
  132.6 1.8 %load.1 = f32[16,4,2176]{2,1,0:T(4,128)S(1)} custom-call(s32[16]{0:T(128)S(1)} %bitcast.18, s32[1]{0:T(128)} %bitcast.14.count_ref, bf16[4,528,256]{2,1,0:T(8,128)(2,1)S(1)} %all_to_all.33.fresh_ref.recv_ref, bf16[16,256,256]{2,1,0:T(8,128)(2,1)S(1)} %bitcast.16), custom_call_target="tpu_custom_call" | custom-call | tf_op jit(solution)/shard_map/load/pallas_call | solution.py:169
  134.4 0.8 convert_element_type.44
  135.2 3.9 %all-to-all-start.5 = ((f16[16,4,2176]{2,1,0:T(4,128)(2,1)}), f16[16,4,2176]{2,1,0:T(4,128)(2,1)S(1)}, u32[]{:S(2)}, u32[]{:S(2)}) async-start(f16[16,4,2176]{2,1,0:T(4,128)(2,1)} %convert_element_type.44), calls=%async_computation.5 | async-start | bytes 557056 | tf_op jit(solution)/shard_map/all_to_all | solution.py:178
  139.1 0.1 pad_add_fusion.place_ref
  139.3 1.3 spectra.1
  140.6 22.8 %all-to-all-done.5 = f16[16,4,2176]{2,1,0:T(4,128)(2,1)S(1)} async-done(((f16[16,4,2176]{2,1,0:T(4,128)(2,1)}), f16[16,4,2176]{2,1,0:T(4,128)(2,1)S(1)}, u32[]{:S(2)}, u32[]{:S(2)}) %all-to-all-start.5) | async-done | bytes 278560 | tf_op jit(solution)/shard_map/all_to_all | solution.py:178
  163.4 0.1 convert_element_type.45
  163.5 0.1 fusion.3
  163.6 0.1 copy.14
  163.7 0.1 copy.15
  163.8 0.2 fusion
  164.0 0.1 copy.17
  164.1 0.1 copy.18
  164.2 0.1 fusion.2
  164.3 0.8 convolution_divide_fusion
  (24 shorter events, 0.3 us)
Async XLA Ops:
  2.2 42.0 %all-to-all-start = ((bf16[16,4,2048]{2,1,0:T(4,128)(2,1)}), bf16[16,4,2048]{2,1,0:T(4,128)(2,1)S(1)}, u32[]{:S(2)}, u32[]{:S(2)}) async-start(bf16[16,4,2048]{2,1,0:T(4,128)(2,1)} %broadcast_in_dim.4), calls=%async_computation | async-start | bytes 524288 | tf_op jit(solution)/shard_map/all_to_all | solution.py:128
  44.1 1.6 copy-start
  45.7 0.7 copy-start.3
  115.6 17.0 %copy-start.1 = (bf16[1,1,16,256,256]{4,3,2,1,0:T(8,128)(2,1)S(1)}, bf16[1,1,16,256,256]{4,3,2,1,0:T(8,128)(2,1)}, u32[]{:S(2)}) copy-start(bf16[1,1,16,256,256]{4,3,2,1,0:T(8,128)(2,1)} %param.5) | copy-start | bytes 6291460
  115.6 16.9 %copy-start.4 = (s32[1,1,16]{2,1,0:T(1,128)S(1)}, s32[1,1,16]{2,1,0:T(1,128)}, u32[]{:S(2)}) copy-start(s32[1,1,16]{2,1,0:T(1,128)} %param.6) | copy-start | bytes 196
  134.4 4.9 %copy-start.2 = (f32[2,8192]{1,0:T(2,128)S(1)}, f32[2,8192]{1,0:T(2,128)}, u32[]{:S(2)}) copy-start(f32[2,8192]{1,0:T(2,128)} %spec_ref.1) | copy-start | bytes 196612
  135.2 28.2 %all-to-all-start.5 = ((f16[16,4,2176]{2,1,0:T(4,128)(2,1)}), f16[16,4,2176]{2,1,0:T(4,128)(2,1)S(1)}, u32[]{:S(2)}, u32[]{:S(2)}) async-start(f16[16,4,2176]{2,1,0:T(4,128)(2,1)} %convert_element_type.44), calls=%async_computation.5 | async-start | bytes 557056 | tf_op jit(solution)/shard_map/all_to_all | solution.py:178
  140.6 23.7 %copy-start.5 = (f32[4,2048]{1,0:T(4,128)S(1)}, f32[4,2048]{1,0:T(4,128)}, u32[]{:S(2)}) copy-start(f32[4,2048]{1,0:T(4,128)} %param.8) | copy-start | bytes 98308

commit v3 on v1

v3 whole, which is shorter than its diff:
```python
import jax
import jax.numpy as jnp
from jax import lax
from jax.experimental import pallas as pl
from jax.experimental.pallas import tpu as pltpu
from jax.sharding import Mesh, PartitionSpec as P

F32, BF16, F16 = jnp.float32, jnp.bfloat16, jnp.float16
PIX = ("zl", "y")
MASS = ("zh", "x", "core")
RANK, TILE, TROWS, TCOLS, CAP = 64, 256, 8, 32, 16
NZ, NY, NMASS = 8, 4, 16
PER = RANK // NMASS
TOP_SCALE = 2.0**-10
GRAM_SCALE = 2.0**-3
TOPS = NZ * RANK
PIXELS = TROWS * TILE
WIDE = PIXELS + 128
VMEM = pl.BlockSpec(memory_space=pltpu.VMEM)
SMEM = pl.BlockSpec(memory_space=pltpu.SMEM)
PARAMS = pltpu.CompilerParams(vmem_limit_bytes=12 << 20)
CONTRACT_LAST = (((1,), (1,)), ((), ()))


def half_precision(x):
    wide = x * 8193.0
    return wide - (wide - x)


def own_kernel(loading_ref, out_ref):
    half = loading_ref[...].astype(BF16)
    for m in range(NMASS // 2):
        out_ref[m] = half


def fetch_kernel(tiles_ref, spec_ref, out_ref, sent_ref, sem):
    copy = pltpu.make_async_copy(tiles_ref, out_ref, sem)
    copy.start()
    sent_ref[...] = half_precision(spec_ref[...])
    copy.wait()


def spec_kernel(meta_ref, load_ref, tiles_ref, sent_ref, out_ref, half_ref, wide_ref):
    for m in range(NMASS):
        wide_ref[pl.ds(PER * m, PER), :] = load_ref[m % 2, m // 2].astype(F32)
    half_ref[...] = wide_ref[...].astype(BF16)
    for y in range(NY):
        out_ref[y, pl.ds(0, TOPS), :] = jnp.zeros((TOPS, TILE), F32)
    count = meta_ref[CAP]
    for s in range(CAP):
        place = meta_ref[s]
        row, col = place // TCOLS, place % TCOLS
        lanes = pl.ds(pl.multiple_of(row * TILE, TILE), TILE)
        product = jnp.dot(half_ref[:, lanes], tiles_ref[s], preferred_element_type=F32) * TOP_SCALE
        rows = pl.ds(pl.multiple_of((col // NY) * RANK, RANK), RANK)
        out_ref[col % NY, rows, :] += jnp.where(s < count, product, 0.0)
    half = half_ref[...]
    gram = lax.dot_general(half, half, CONTRACT_LAST, preferred_element_type=F32) * GRAM_SCALE
    packed = jnp.concatenate([gram[16 * i : 16 * i + 16, :] for i in range(4)], axis=1)
    for y in range(NY):
        for z in range(NZ):
            c = z * NY + y
            out_ref[y, pl.ds(TOPS + 2 * z, 2), :] = sent_ref[:, pl.ds(c * TILE, TILE)]
        out_ref[y, pl.ds(TOPS + 2 * NZ, 16), :] = packed


def update_kernel(sums_ref, spec_ref, out_ref):
    packed = sums_ref[pl.ds(RANK, 16), :] * (TOP_SCALE / GRAM_SCALE)
    gram = jnp.concatenate([packed[:, RANK * i : RANK * i + RANK] for i in range(4)], axis=0)
    spec = spec_ref[...]
    bottom = jnp.dot(gram, spec.astype(BF16).astype(F32), precision=lax.Precision.HIGHEST, preferred_element_type=F32)
    new = spec * sums_ref[pl.ds(0, RANK), :] / bottom
    fresh = new.astype(BF16)
    rest = new - fresh.astype(F32)
    for z in range(NZ):
        out_ref[z, pl.ds(0, RANK), :] = fresh
        out_ref[z, pl.ds(RANK, 8), :] = rest[8 * z : 8 * z + 8, :].astype(BF16)


def spread_kernel(in_ref, out_ref):
    for y in range(NY):
        for z in range(NZ):
            out_ref[y, pl.ds(z * RANK, RANK), :] = in_ref[z, pl.ds(0, RANK), :]
    for z in range(NZ):
        rest = in_ref[z, pl.ds(RANK, 8), :].astype(F32)
        for y in range(NY):
            out_ref[y, pl.ds(TOPS + 2 * z, 2), :] = rest[2 * y : 2 * y + 2, :].astype(BF16)


def load_kernel(meta_ref, fresh_ref, tiles_ref, out_ref, acc_ref):
    acc_ref[...] = jnp.zeros_like(acc_ref)
    count = meta_ref[CAP]
    for s in range(CAP):
        place = meta_ref[s]
        row, col = place // TCOLS, place % TCOLS
        rows = pl.ds(pl.multiple_of((col // NY) * RANK, RANK), RANK)
        block = fresh_ref[col % NY, rows, :]
        product = lax.dot_general(block, tiles_ref[s], CONTRACT_LAST, preferred_element_type=F32)
        lanes = pl.ds(pl.multiple_of(row * TILE, TILE), TILE)
        acc_ref[:, lanes] += jnp.where(s < count, product, 0.0)
    gram = jnp.zeros((RANK, RANK), F32)
    for y in range(NY):
        for z in range(NZ):
            block = fresh_ref[y, pl.ds(z * RANK, RANK), :]
            gram = gram + lax.dot_general(block, block, CONTRACT_LAST, preferred_element_type=F32)
    top = acc_ref[...]
    tail = jnp.concatenate([gram, jnp.zeros((RANK, RANK), F32)], axis=1)
    for m in range(NMASS):
        rows = pl.ds(PER * (m // 2), PER)
        out_ref[m % 2, rows, pl.ds(0, PIXELS)] = top[PER * m : PER * m + PER, :]
        out_ref[m % 2, rows, pl.ds(PIXELS, 128)] = tail[PER * m : PER * m + PER, :]


def encode_kernel(in_ref, out_ref):
    total = in_ref[0] + in_ref[1]

    def exponent(x):
        return jnp.floor(jnp.log2(jnp.maximum(jnp.max(x, axis=1, keepdims=True), 1e-30))) - 13.0

    top, gram = total[:, :PIXELS], total[:, PIXELS : PIXELS + RANK]
    top_exp, gram_exp = exponent(top), exponent(gram)
    top = top * jnp.exp2(-top_exp)
    gram = gram * jnp.exp2(-gram_exp)
    lane = lax.broadcasted_iota(jnp.int32, gram.shape, 1)
    tail = jnp.where(lane == 0, top_exp, jnp.where(lane == 1, gram_exp, 0.0))
    tail = jnp.concatenate([gram, tail], axis=1)
    for m in range(NMASS // 2):
        out_ref[m, :, pl.ds(0, PIXELS)] = top[PER * m : PER * m + PER, :]
        out_ref[m, :, pl.ds(PIXELS, 128)] = tail[PER * m : PER * m + PER, :]


def final_kernel(part_ref, half_ref, loading_ref, out_ref):
    top = jnp.zeros((PER, PIXELS), F32)
    gram = jnp.zeros((PER, RANK), F32)
    for m in range(NMASS // 2):
        tail = part_ref[m, :, pl.ds(PIXELS, 128)]
        top = top + part_ref[m, :, pl.ds(0, PIXELS)] * jnp.exp2(tail[:, RANK : RANK + 1])
        gram = gram + tail[:, :RANK] * jnp.exp2(tail[:, RANK + 1 : RANK + 2])
    bottom = jnp.dot(gram, half_ref[...].astype(F32), precision=lax.Precision.HIGHEST, preferred_element_type=F32)
    out_ref[...] = loading_ref[...] * top / bottom


def spectra_kernel(place_ref, recv_ref, spec_ref, out_ref):
    zl, yl = place_ref[0], place_ref[1]
    for z in range(NZ):
        for y in range(NY):
            c = z * NY + y
            eight = recv_ref[y, pl.ds(pl.multiple_of(z * RANK + 8 * zl, 8), 8), :].astype(F32)
            two = eight[0:2, :]
            for k in range(1, NY):
                two = jnp.where(yl == k, eight[2 * k : 2 * k + 2, :], two)
            rest = recv_ref[y, pl.ds(TOPS + 2 * z, 2), :].astype(F32)
            cols = pl.ds(c * TILE, TILE)
            spec = spec_ref[:, cols]
            out_ref[:, cols] = (two + rest) * (spec / half_precision(spec))


def near(x):
    return pltpu.with_memory_space_constraint(x, pltpu.VMEM)


def call(body, out, *operands, scratch=(), pinned=True):
    specs = [SMEM if x.dtype == jnp.int32 else VMEM for x in operands]
    return pl.pallas_call(
        body,
        out_shape=out,
        in_specs=specs,
        out_specs=jax.tree.map(lambda _: VMEM, out),
        scratch_shapes=scratch,
        compiler_params=PARAMS,
        name=body.__name__,
    )(*[near(x) if pinned and x.dtype != jnp.int32 else x for x in operands])


def local(tiles, tile_pos, kept_tile_count, loading, spectra):
    tiles = tiles[0, 0]
    meta = jnp.concatenate([tile_pos[0, 0], kept_tile_count[0]])

    load = call(own_kernel, pltpu.VMEM((NMASS // 2, PER, PIXELS), BF16), loading, pinned=False)
    load = lax.all_to_all(load, ("zh", "x"), 0, 0, tiled=True)
    load = lax.all_gather(load, "core", axis=0, tiled=False)
    tiles, sent = pl.pallas_call(
        fetch_kernel,
        out_shape=(pltpu.VMEM(tiles.shape, BF16), pltpu.VMEM(spectra.shape, F32)),
        in_specs=[pl.BlockSpec(memory_space=pl.ANY), VMEM],
        out_specs=(VMEM, VMEM),
        scratch_shapes=[pltpu.SemaphoreType.DMA],
        compiler_params=PARAMS,
        name="fetch_kernel",
    )(tiles, spectra)

    out, half = call(
        spec_kernel,
        (pltpu.VMEM((NY, TOPS + 32, TILE), F32), pltpu.VMEM((RANK, PIXELS), BF16)),
        meta, load, tiles, sent,
        scratch=[pltpu.VMEM((RANK, PIXELS), F32)],
    )
    part = lax.all_to_all(out.astype(F16), "y", 0, 0, tiled=True)
    tops = part[:, :TOPS].astype(F32).sum(0).astype(F16).reshape(NZ, RANK, TILE)
    old = part[:, TOPS : TOPS + 2 * NZ].reshape(NY, NZ, 2, TILE).transpose(1, 0, 2, 3).reshape(NZ, 8, TILE)
    gram = part[:, TOPS + 2 * NZ :].astype(F32).sum(0).astype(F16)
    gram = jnp.broadcast_to(gram[None], (NZ, 16, TILE))
    part = lax.all_to_all(jnp.concatenate([tops, old, gram], axis=1), "zl", 0, 0, tiled=True)
    wide = part.astype(F32)
    sums = jnp.concatenate([wide[:, :RANK].sum(0), wide[:, RANK + 8 :].sum(0)], axis=0)
    old = wide[:, RANK : RANK + 8].reshape(RANK, TILE)

    fresh = call(update_kernel, pltpu.VMEM((NZ, RANK + 8, TILE), BF16), sums, old)
    fresh = lax.all_to_all(fresh, "zl", 0, 0, tiled=True)
    fresh = call(spread_kernel, pltpu.VMEM((NY, TOPS + 16, TILE), BF16), fresh)
    fresh = lax.all_to_all(fresh, "y", 0, 0, tiled=True)

    out = call(
        load_kernel,
        pltpu.VMEM((2, RANK // 2, WIDE), F32),
        meta, fresh, tiles,
        scratch=[pltpu.VMEM((RANK, PIXELS), F32)],
    )
    part = lax.all_to_all(out, "core", 0, 0, tiled=True)
    part = call(encode_kernel, pltpu.VMEM((NMASS // 2, PER, WIDE), F32), part)
    part = lax.all_to_all(part.astype(F16), ("zh", "x"), 0, 0, tiled=True).astype(F32)

    place = jnp.stack([lax.axis_index("zl"), lax.axis_index("y")]).astype(jnp.int32)
    spectra_new = call(spectra_kernel, jax.ShapeDtypeStruct(spectra.shape, F32), place, fresh, spectra)
    loading_new = call(final_kernel, jax.ShapeDtypeStruct(loading.shape, F32), part, half, loading)
    return (loading_new, spectra_new)


def solution(mesh):
    fine = Mesh(mesh.devices.reshape(NZ, NY, 2, 4, 2), PIX + MASS)
    return jax.shard_map(
        local,
        mesh=fine,
        in_specs=(P(PIX, MASS, None, None, None), P(PIX, MASS, None), P(PIX, MASS), P(MASS, PIX), P(PIX, MASS)),
        out_specs=(P(MASS, PIX), P(PIX, MASS)),
        check_vma=False,
    )
```

time: 179 us -> 155 us (0.87)
  waiting for transfers between devices: 44.5 us -> 30.8 us
  Pallas kernels: 13.7 us -> 6.66 us
  other arithmetic: 8.1 us -> 3.18 us
  blocking collectives: 85.7 us -> 88.7 us
    all_to_all x2, waiting for transfers between devices: 44.5 us -> 30.8 us  [the longest x1 15.6 us: local(): load = lax.all_to_all(load, ('zh', 'x'), 0, 0, tiled=True)]
    pallas_call x5 -> x9, Pallas kernels: 13.7 us -> 6.66 us  [the longest x8 6.5 us: call(): pl.pallas_call(body, out_shape=out, in_specs=specs, out_specs=jax.tree.ma...]
    all_to_all x0 -> x1, blocking collectives: none -> 4.29 us  [local(): part = lax.all_to_all(out, 'core', 0, 0, tiled=True)]
    unnamed x6 -> x12, local copies, waits for them, and re-layouts: 0.7 us -> 3.19 us
    convert_element_type x3 -> x2, other arithmetic: 2.76 us -> 0.76 us  [the longest x1 0.71 us: local(): part.astype(F16)]
    all_gather x0 -> x1, blocking collectives: none -> 1.98 us  [local(): load = lax.all_gather(load, 'core', axis=0, tiled=False)]
    all_to_all x1, blocking collectives: 18.7 us -> 16.8 us  [local(): fresh = lax.all_to_all(fresh, 'y', 0, 0, tiled=True)]
  transfers between devices with their start and end apart: 2 -> 2, of which waited for: 2 -> 2; matrix products, arithmetic and copies ran while one was open for 1% -> 0% of each run, Pallas kernels for 1% -> 1%
where the time goes in v3:
time: 155 us; the launch traced here: 154 us
  blocking collectives  88.7 us (57%)
  waiting for transfers between devices  30.8 us (20%)
  starting transfers between devices  20 us (13%)
  Pallas kernels  6.66 us (4%)
  local copies, waits for them, and re-layouts  3.29 us (2%)
  other arithmetic  3.18 us (2%)
    all_to_all x1, blocking collectives, local(): fresh = lax.all_to_all(fresh, 'zl', 0, 0, tiled=True)  22.8 us
    all_to_all x1, blocking collectives, local(): lax.all_to_all(jnp.concatenate([tops, old, gram], axis=1), 'zl', 0, 0, ti...  22.5 us
    all_to_all x1, blocking collectives, local(): part = lax.all_to_all(out.astype(F16), 'y', 0, 0, tiled=True)  20.4 us
    all_to_all x1, blocking collectives, local(): fresh = lax.all_to_all(fresh, 'y', 0, 0, tiled=True)  16.8 us
    all_to_all x1, starting transfers between devices, local(): load = lax.all_to_all(load, ('zh', 'x'), 0, 0, tiled=True)  16.7 us
    all_to_all x1, waiting for transfers between devices, local(): load = lax.all_to_all(load, ('zh', 'x'), 0, 0, tiled=True)  15.6 us
    all_to_all x1, waiting for transfers between devices, local(): lax.all_to_all(part.astype(F16), ('zh', 'x'), 0, 0, tiled=True).astype(F32)  15.2 us
    pallas_call x8, Pallas kernels, call(): pl.pallas_call(body, out_shape=out, in_specs=specs, out_specs=jax.tree.ma...  6.5 us
  transfers between devices with their start and end apart: 2, of which 2 were waited for; matrix products, arithmetic and copies ran while one was open for 0% of the time, Pallas kernels for 1%

profile of v3, /device:TPU:32, one launch (start us, length us, event | category | flops | bytes accessed | tf_op | source)
XLA Modules:
  0.0 154.1 jit_solution(15507968947949506265)
XLA Ops:
  0.6 0.0 copy-start.3
  0.6 0.7 copy-done.3
  1.4 0.7 own_kernel.1
  2.1 16.7 %all-to-all-start = ((bf16[8,4,2048]{2,1,0:T(4,128)(2,1)}), bf16[8,4,2048]{2,1,0:T(4,128)(2,1)S(1)}, u32[]{:S(2)}, u32[]{:S(2)}) async-start(bf16[8,4,2048]{2,1,0:T(4,128)(2,1)} %own_kernel.1), calls=%async_computation | async-start | bytes 262144 | tf_op jit(solution)/shard_map/all_to_all | solution.py:180
  19.4 0.0 copy-start
  19.4 1.6 %copy-done = bf16[1,1,16,256,256]{4,3,2,1,0:T(8,128)(2,1)S(1)} copy-done((bf16[1,1,16,256,256]{4,3,2,1,0:T(8,128)(2,1)S(1)}, bf16[1,1,16,256,256]{4,3,2,1,0:T(8,128)(2,1)}, u32[]{:S(2)}) %copy-start) | copy-done | bytes 2097176
  21.0 0.8 copy-done.1
  21.8 0.2 fetch_kernel.1
  22.0 0.1 pad_add_fusion.meta_ref
  22.1 15.6 %all-to-all-done = bf16[8,4,2048]{2,1,0:T(4,128)(2,1)S(1)} async-done(((bf16[8,4,2048]{2,1,0:T(4,128)(2,1)}), bf16[8,4,2048]{2,1,0:T(4,128)(2,1)S(1)}, u32[]{:S(2)}, u32[]{:S(2)}) %all-to-all-start) | async-done | bytes 131104 | tf_op jit(solution)/shard_map/all_to_all | solution.py:180
  37.7 2.0 %all-gather = bf16[16,4,2048]{2,1,0:T(4,128)(2,1)S(1)} all-gather(bf16[8,4,2048]{2,1,0:T(4,128)(2,1)S(1)} %all-to-all-done), channel_id=2, replica_groups=mesh['zl'=8,'y'=4,'zh'=2,'x'=4,'core'=2] {'core'}, dimensions={0}, use_global_device_ids=true | all-gather | bytes 393216 | tf_op jit(solution)/shard_map/all_gather | solution.py:181
  39.7 1.3 spec_kernel.1
  41.0 0.2 convert_element_type.32
  41.2 20.4 %all_to_all.35 = f16[4,544,256]{2,1,0:T(8,128)(2,1)S(1)} all-to-all(f16[4,544,256]{2,1,0:T(8,128)(2,1)S(1)} %convert_element_type.32), channel_id=1, replica_groups=mesh['zl'=8,'y'=4,'zh'=2,'x'=4,'core'=2] {'y'}, dimensions={0} | all-to-all | bytes 2228224 | tf_op jit(solution)/shard_map/all_to_all | solution.py:198
  61.6 0.1 convert_reduce_fusion
  61.7 0.7 convert_element_type.34
  62.6 1.1 pad_maximum_fusion
  63.7 22.5 %all_to_all.36 = f16[8,88,256]{2,1,0:T(8,128)(2,1)S(1)} all-to-all(f16[8,88,256]{2,1,0:T(8,128)(2,1)S(1)} %pad_maximum_fusion), channel_id=1, replica_groups=mesh['zl'=8,'y'=4,'zh'=2,'x'=4,'core'=2] {'zl'}, dimensions={0} | all-to-all | bytes 720896 | tf_op jit(solution)/shard_map/all_to_all | solution.py:203
  86.3 0.3 update_kernel.1
  86.6 22.8 %all_to_all.37.in_ref = bf16[8,72,256]{2,1,0:T(8,128)(2,1)S(1)} all-to-all(bf16[8,72,256]{2,1,0:T(8,128)(2,1)S(1)} %update_kernel.1), channel_id=1, replica_groups=mesh['zl'=8,'y'=4,'zh'=2,'x'=4,'core'=2] {'zl'}, dimensions={0} | all-to-all | bytes 589824 | tf_op jit(solution)/shard_map/all_to_all | solution.py:209
  109.4 0.1 spread_kernel.1
  109.4 16.8 %all_to_all.38.fresh_ref.recv_ref = bf16[4,528,256]{2,1,0:T(8,128)(2,1)S(1)} all-to-all(bf16[4,528,256]{2,1,0:T(8,128)(2,1)S(1)} %spread_kernel.1), channel_id=1, replica_groups=mesh['zl'=8,'y'=4,'zh'=2,'x'=4,'core'=2] {'y'}, dimensions={0} | all-to-all | bytes 2162688 | tf_op jit(solution)/shard_map/all_to_all | solution.py:211
  126.2 1.6 %load_kernel.1 = f32[2,32,2176]{2,1,0:T(8,128)S(1)} custom-call(s32[17]{0:T(128)S(1)} %pad_add_fusion.meta_ref, bf16[4,528,256]{2,1,0:T(8,128)(2,1)S(1)} %all_to_all.38.fresh_ref.recv_ref, bf16[16,256,256]{2,1,0:T(8,128)(2,1)S(1)} %get-tuple-element.6.tiles_ref), custom_call_target="tpu_custom_call" | custom-call | tf_op jit(solution)/shard_map/load_kernel/pallas_call | solution.py:164
  127.9 0.0 copy-start.2
  127.9 4.3 %all_to_all.39.in_ref = f32[2,32,2176]{2,1,0:T(8,128)S(1)} all-to-all(f32[2,32,2176]{2,1,0:T(8,128)S(1)} %load_kernel.1), channel_id=1, replica_groups=mesh['zl'=8,'y'=4,'zh'=2,'x'=4,'core'=2] {'core'}, dimensions={0} | all-to-all | bytes 1114112 | tf_op jit(solution)/shard_map/all_to_all | solution.py:219
  132.2 0.2 encode_kernel.1
  132.4 0.7 convert_element_type.39
  133.1 3.4 %all-to-all-start.6 = ((f16[8,4,2176]{2,1,0:T(4,128)(2,1)}), f16[8,4,2176]{2,1,0:T(4,128)(2,1)S(1)}, u32[]{:S(2)}, u32[]{:S(2)}) async-start(f16[8,4,2176]{2,1,0:T(4,128)(2,1)} %convert_element_type.39), calls=%async_computation.6 | async-start | bytes 278528 | tf_op jit(solution)/shard_map/all_to_all | solution.py:221
  136.5 0.1 pad_add_fusion.1.place_ref
  136.6 1.3 spectra_kernel.1
  137.9 15.2 %all-to-all-done.6 = f16[8,4,2176]{2,1,0:T(4,128)(2,1)S(1)} async-done(((f16[8,4,2176]{2,1,0:T(4,128)(2,1)}), f16[8,4,2176]{2,1,0:T(4,128)(2,1)S(1)}, u32[]{:S(2)}, u32[]{:S(2)}) %all-to-all-start.6) | async-done | bytes 139296 | tf_op jit(solution)/shard_map/all_to_all | solution.py:221
  153.1 1.0 final_kernel.1
  (19 shorter events, 0.3 us)
Async XLA Ops:
  0.6 0.8 copy-start.3
  2.1 35.6 %all-to-all-start = ((bf16[8,4,2048]{2,1,0:T(4,128)(2,1)}), bf16[8,4,2048]{2,1,0:T(4,128)(2,1)S(1)}, u32[]{:S(2)}, u32[]{:S(2)}) async-start(bf16[8,4,2048]{2,1,0:T(4,128)(2,1)} %own_kernel.1), calls=%async_computation | async-start | bytes 262144 | tf_op jit(solution)/shard_map/all_to_all | solution.py:180
  18.7 3.3 %copy-start.5 = (s32[1,1,16]{2,1,0:T(1,128)S(1)}, s32[1,1,16]{2,1,0:T(1,128)}, u32[]{:S(2)}) copy-start(s32[1,1,16]{2,1,0:T(1,128)} %param.6) | copy-start | bytes 196
  19.4 1.6 %copy-start = (bf16[1,1,16,256,256]{4,3,2,1,0:T(8,128)(2,1)S(1)}, bf16[1,1,16,256,256]{4,3,2,1,0:T(8,128)(2,1)}, u32[]{:S(2)}) copy-start(bf16[1,1,16,256,256]{4,3,2,1,0:T(8,128)(2,1)} %param.5) | copy-start | bytes 6291460
  21.0 0.8 copy-start.1
  127.9 8.7 %copy-start.2 = (f32[2,8192]{1,0:T(2,128)S(1)}, f32[2,8192]{1,0:T(2,128)}, u32[]{:S(2)}) copy-start(f32[2,8192]{1,0:T(2,128)} %spec_ref.3) | copy-start | bytes 196612
  132.4 20.7 %copy-start.4 = (f32[4,2048]{1,0:T(4,128)S(1)}, f32[4,2048]{1,0:T(4,128)}, u32[]{:S(2)}) copy-start(f32[4,2048]{1,0:T(4,128)} %loading_ref.3) | copy-start | bytes 98308
  133.1 20.0 %all-to-all-start.6 = ((f16[8,4,2176]{2,1,0:T(4,128)(2,1)}), f16[8,4,2176]{2,1,0:T(4,128)(2,1)S(1)}, u32[]{:S(2)}, u32[]{:S(2)}) async-start(f16[8,4,2176]{2,1,0:T(4,128)(2,1)} %convert_element_type.39), calls=%async_computation.6 | async-start | bytes 278528 | tf_op jit(solution)/shard_map/all_to_all | solution.py:221

commit v4 on v3

--- a/solution.py
+++ b/solution.py
@@ -6,10 +6,11 @@
 from jax.sharding import Mesh, PartitionSpec as P
 
 F32, BF16, F16 = jnp.float32, jnp.bfloat16, jnp.float16
-PIX = ("zl", "y")
+PIX = ("p", "q")
 MASS = ("zh", "x", "core")
 RANK, TILE, TROWS, TCOLS, CAP = 64, 256, 8, 32, 16
-NZ, NY, NMASS = 8, 4, 16
+NZ, NY, NMASS = 4, 8, 16
+OWN = RANK // NZ
 PER = RANK // NMASS
 TOP_SCALE = 2.0**-10
 GRAM_SCALE = 2.0**-3
@@ -64,17 +65,37 @@
         out_ref[y, pl.ds(TOPS + 2 * NZ, 16), :] = packed
 
 
-def update_kernel(sums_ref, spec_ref, out_ref):
-    packed = sums_ref[pl.ds(RANK, 16), :] * (TOP_SCALE / GRAM_SCALE)
+def middle_kernel(in_ref, out_ref):
+    gram = in_ref[0, pl.ds(TOPS + 2 * NZ, 16), :]
+    for y in range(1, NY):
+        gram = gram + in_ref[y, pl.ds(TOPS + 2 * NZ, 16), :]
+    for z in range(NZ):
+        rows = pl.ds(z * RANK, RANK)
+        top = in_ref[0, rows, :]
+        for y in range(1, NY):
+            top = top + in_ref[y, rows, :]
+        out_ref[z, pl.ds(0, RANK), :] = top
+        for y in range(NY):
+            out_ref[z, pl.ds(RANK + 2 * y, 2), :] = in_ref[y, pl.ds(TOPS + 2 * z, 2), :]
+        out_ref[z, pl.ds(RANK + OWN, 16), :] = gram
+
+
+def update_kernel(in_ref, out_ref):
+    packed = in_ref[0, pl.ds(RANK + OWN, 16), :]
+    top = in_ref[0, pl.ds(0, RANK), :]
+    for z in range(1, NZ):
+        packed = packed + in_ref[z, pl.ds(RANK + OWN, 16), :]
+        top = top + in_ref[z, pl.ds(0, RANK), :]
+    packed = packed * (TOP_SCALE / GRAM_SCALE)
     gram = jnp.concatenate([packed[:, RANK * i : RANK * i + RANK] for i in range(4)], axis=0)
-    spec = spec_ref[...]
+    spec = jnp.concatenate([in_ref[z, pl.ds(RANK, OWN), :] for z in range(NZ)], axis=0)
     bottom = jnp.dot(gram, spec.astype(BF16).astype(F32), precision=lax.Precision.HIGHEST, preferred_element_type=F32)
-    new = spec * sums_ref[pl.ds(0, RANK), :] / bottom
+    new = spec * top / bottom
     fresh = new.astype(BF16)
     rest = new - fresh.astype(F32)
     for z in range(NZ):
         out_ref[z, pl.ds(0, RANK), :] = fresh
-        out_ref[z, pl.ds(RANK, 8), :] = rest[8 * z : 8 * z + 8, :].astype(BF16)
+        out_ref[z, pl.ds(RANK, OWN), :] = rest[OWN * z : OWN * z + OWN, :].astype(BF16)
 
 
 def spread_kernel(in_ref, out_ref):
@@ -82,7 +103,7 @@
         for z in range(NZ):
             out_ref[y, pl.ds(z * RANK, RANK), :] = in_ref[z, pl.ds(0, RANK), :]
     for z in range(NZ):
-        rest = in_ref[z, pl.ds(RANK, 8), :].astype(F32)
+        rest = in_ref[z, pl.ds(RANK, OWN), :].astype(F32)
         for y in range(NY):
             out_ref[y, pl.ds(TOPS + 2 * z, 2), :] = rest[2 * y : 2 * y + 2, :].astype(BF16)
 
@@ -145,10 +166,10 @@
     for z in range(NZ):
         for y in range(NY):
             c = z * NY + y
-            eight = recv_ref[y, pl.ds(pl.multiple_of(z * RANK + 8 * zl, 8), 8), :].astype(F32)
-            two = eight[0:2, :]
+            own = recv_ref[y, pl.ds(pl.multiple_of(z * RANK + OWN * zl, OWN), OWN), :].astype(F32)
+            two = own[0:2, :]
             for k in range(1, NY):
-                two = jnp.where(yl == k, eight[2 * k : 2 * k + 2, :], two)
+                two = jnp.where(yl == k, own[2 * k : 2 * k + 2, :], two)
             rest = recv_ref[y, pl.ds(TOPS + 2 * z, 2), :].astype(F32)
             cols = pl.ds(c * TILE, TILE)
             spec = spec_ref[:, cols]
@@ -191,24 +212,18 @@
 
     out, half = call(
         spec_kernel,
-        (pltpu.VMEM((NY, TOPS + 32, TILE), F32), pltpu.VMEM((RANK, PIXELS), BF16)),
+        (pltpu.VMEM((NY, TOPS + 2 * NZ + 16, TILE), F32), pltpu.VMEM((RANK, PIXELS), BF16)),
         meta, load, tiles, sent,
         scratch=[pltpu.VMEM((RANK, PIXELS), F32)],
     )
-    part = lax.all_to_all(out.astype(F16), "y", 0, 0, tiled=True)
-    tops = part[:, :TOPS].astype(F32).sum(0).astype(F16).reshape(NZ, RANK, TILE)
-    old = part[:, TOPS : TOPS + 2 * NZ].reshape(NY, NZ, 2, TILE).transpose(1, 0, 2, 3).reshape(NZ, 8, TILE)
-    gram = part[:, TOPS + 2 * NZ :].astype(F32).sum(0).astype(F16)
-    gram = jnp.broadcast_to(gram[None], (NZ, 16, TILE))
-    part = lax.all_to_all(jnp.concatenate([tops, old, gram], axis=1), "zl", 0, 0, tiled=True)
-    wide = part.astype(F32)
-    sums = jnp.concatenate([wide[:, :RANK].sum(0), wide[:, RANK + 8 :].sum(0)], axis=0)
-    old = wide[:, RANK : RANK + 8].reshape(RANK, TILE)
-
-    fresh = call(update_kernel, pltpu.VMEM((NZ, RANK + 8, TILE), BF16), sums, old)
-    fresh = lax.all_to_all(fresh, "zl", 0, 0, tiled=True)
-    fresh = call(spread_kernel, pltpu.VMEM((NY, TOPS + 16, TILE), BF16), fresh)
-    fresh = lax.all_to_all(fresh, "y", 0, 0, tiled=True)
+    part = lax.all_to_all(out.astype(F16), "q", 0, 0, tiled=True)
+    part = call(middle_kernel, pltpu.VMEM((NZ, RANK + OWN + 16, TILE), F32), part.astype(F32))
+    part = lax.all_to_all(part.astype(F16), "p", 0, 0, tiled=True)
+
+    fresh = call(update_kernel, pltpu.VMEM((NZ, RANK + OWN, TILE), BF16), part.astype(F32))
+    fresh = lax.all_to_all(fresh, "p", 0, 0, tiled=True)
+    fresh = call(spread_kernel, pltpu.VMEM((NY, TOPS + 2 * NZ, TILE), BF16), fresh)
+    fresh = lax.all_to_all(fresh, "q", 0, 0, tiled=True)
 
     out = call(
         load_kernel,
@@ -220,7 +235,7 @@
     part = call(encode_kernel, pltpu.VMEM((NMASS // 2, PER, WIDE), F32), part)
     part = lax.all_to_all(part.astype(F16), ("zh", "x"), 0, 0, tiled=True).astype(F32)
 
-    place = jnp.stack([lax.axis_index("zl"), lax.axis_index("y")]).astype(jnp.int32)
+    place = jnp.stack([lax.axis_index("p"), lax.axis_index("q")]).astype(jnp.int32)
     spectra_new = call(spectra_kernel, jax.ShapeDtypeStruct(spectra.shape, F32), place, fresh, spectra)
     loading_new = call(final_kernel, jax.ShapeDtypeStruct(loading.shape, F32), part, half, loading)
     return (loading_new, spectra_new)

time: 155 us -> 141 us (0.910)
  blocking collectives: 88.7 us -> 75.8 us
  other arithmetic: 3.18 us -> 1.34 us
    all_to_all x4, blocking collectives: 82.4 us -> 69.5 us  [the longest x1 21.5 us: local(): part = lax.all_to_all(out.astype(F16), 'q', 0, 0, tiled=True)]
    pallas_call x8 -> x9, Pallas kernels: 6.5 us -> 6.68 us  [call(): pl.pallas_call(body, out_shape=out, in_specs=specs, out_specs=jax.tree.ma...]
where the time goes in v4:
time: 141 us
  blocking collectives  75.8 us (54%)
  waiting for transfers between devices  32.2 us (23%)
  starting transfers between devices  20 us (14%)
  Pallas kernels  6.84 us (5%)
  local copies, waits for them, and re-layouts  3.19 us (2%)
  between operations  1.42 us (1%)
    all_to_all x1, blocking collectives, local(): part = lax.all_to_all(out.astype(F16), 'q', 0, 0, tiled=True)  21.5 us
    all_to_all x1, blocking collectives, local(): fresh = lax.all_to_all(fresh, 'q', 0, 0, tiled=True)  17.9 us
    all_to_all x1, starting transfers between devices, local(): load = lax.all_to_all(load, ('zh', 'x'), 0, 0, tiled=True)  16.7 us
    all_to_all x1, waiting for transfers between devices, local(): lax.all_to_all(part.astype(F16), ('zh', 'x'), 0, 0, tiled=True).astype(F32)  16.6 us
    all_to_all x1, blocking collectives, local(): part = lax.all_to_all(part.astype(F16), 'p', 0, 0, tiled=True)  16 us
    all_to_all x1, waiting for transfers between devices, local(): load = lax.all_to_all(load, ('zh', 'x'), 0, 0, tiled=True)  15.6 us
    all_to_all x1, blocking collectives, local(): fresh = lax.all_to_all(fresh, 'p', 0, 0, tiled=True)  14.2 us
    pallas_call x9, Pallas kernels, call(): pl.pallas_call(body, out_shape=out, in_specs=specs, out_specs=jax.tree.ma...  6.68 us
  transfers between devices with their start and end apart: 2, of which 2 were waited for; matrix products, arithmetic and copies ran while one was open for 0% of the time, Pallas kernels for 1%

profile of v4, /device:TPU:32, one launch (start us, length us, event | category | flops | bytes accessed | tf_op | source)
XLA Modules:
  0.0 140.8 jit_solution(11522698504248982326)
XLA Ops:
  0.6 0.0 copy-start.3
  0.6 0.7 copy-done.3
  1.4 0.7 own_kernel.1
  2.0 16.7 %all-to-all-start = ((bf16[8,4,2048]{2,1,0:T(4,128)(2,1)}), bf16[8,4,2048]{2,1,0:T(4,128)(2,1)S(1)}, u32[]{:S(2)}, u32[]{:S(2)}) async-start(bf16[8,4,2048]{2,1,0:T(4,128)(2,1)} %own_kernel.1), calls=%async_computation | async-start | bytes 262144 | tf_op jit(solution)/shard_map/all_to_all | solution.py:201
  19.3 0.0 copy-start
  19.4 1.6 %copy-done = bf16[1,1,16,256,256]{4,3,2,1,0:T(8,128)(2,1)S(1)} copy-done((bf16[1,1,16,256,256]{4,3,2,1,0:T(8,128)(2,1)S(1)}, bf16[1,1,16,256,256]{4,3,2,1,0:T(8,128)(2,1)}, u32[]{:S(2)}) %copy-start) | copy-done | bytes 2097176
  20.9 0.8 copy-done.1
  21.8 0.2 fetch_kernel.1
  22.0 0.1 pad_add_fusion.meta_ref
  22.0 15.6 %all-to-all-done = bf16[8,4,2048]{2,1,0:T(4,128)(2,1)S(1)} async-done(((bf16[8,4,2048]{2,1,0:T(4,128)(2,1)}), bf16[8,4,2048]{2,1,0:T(4,128)(2,1)S(1)}, u32[]{:S(2)}, u32[]{:S(2)}) %all-to-all-start) | async-done | bytes 131104 | tf_op jit(solution)/shard_map/all_to_all | solution.py:201
  37.7 2.0 %all-gather = bf16[16,4,2048]{2,1,0:T(4,128)(2,1)S(1)} all-gather(bf16[8,4,2048]{2,1,0:T(4,128)(2,1)S(1)} %all-to-all-done), channel_id=2, replica_groups=mesh['p'=4,'q'=8,'zh'=2,'x'=4,'core'=2] {'core'}, dimensions={0}, use_global_device_ids=true | all-gather | bytes 393216 | tf_op jit(solution)/shard_map/all_gather | solution.py:202
  39.6 1.3 spec_kernel.1
  41.0 0.2 convert_element_type.18
  41.2 21.5 %all_to_all.35 = f16[8,280,256]{2,1,0:T(8,128)(2,1)S(1)} all-to-all(f16[8,280,256]{2,1,0:T(8,128)(2,1)S(1)} %convert_element_type.18), channel_id=1, replica_groups=mesh['p'=4,'q'=8,'zh'=2,'x'=4,'core'=2] {'q'}, dimensions={0} | all-to-all | bytes 2293760 | tf_op jit(solution)/shard_map/all_to_all | solution.py:219
  62.7 0.2 convert_element_type.19.in_ref
  62.8 0.1 middle_kernel.1
  63.0 16.0 %all_to_all.36 = f16[4,96,256]{2,1,0:T(8,128)(2,1)S(1)} all-to-all(f16[4,96,256]{2,1,0:T(8,128)(2,1)S(1)} %convert_element_type.20), channel_id=1, replica_groups=mesh['p'=4,'q'=8,'zh'=2,'x'=4,'core'=2] {'p'}, dimensions={0} | all-to-all | bytes 393216 | tf_op jit(solution)/shard_map/all_to_all | solution.py:221
  79.0 0.3 update_kernel.1
  79.3 14.2 %all_to_all.37.in_ref = bf16[4,80,256]{2,1,0:T(8,128)(2,1)S(1)} all-to-all(bf16[4,80,256]{2,1,0:T(8,128)(2,1)S(1)} %update_kernel.1), channel_id=1, replica_groups=mesh['p'=4,'q'=8,'zh'=2,'x'=4,'core'=2] {'p'}, dimensions={0} | all-to-all | bytes 327680 | tf_op jit(solution)/shard_map/all_to_all | solution.py:224
  93.5 0.1 spread_kernel.1
  93.6 17.9 %all_to_all.38.fresh_ref.recv_ref = bf16[8,264,256]{2,1,0:T(8,128)(2,1)S(1)} all-to-all(bf16[8,264,256]{2,1,0:T(8,128)(2,1)S(1)} %spread_kernel.1), channel_id=1, replica_groups=mesh['p'=4,'q'=8,'zh'=2,'x'=4,'core'=2] {'q'}, dimensions={0} | all-to-all | bytes 2162688 | tf_op jit(solution)/shard_map/all_to_all | solution.py:226
  111.5 1.6 %load_kernel.1 = f32[2,32,2176]{2,1,0:T(8,128)S(1)} custom-call(s32[17]{0:T(128)S(1)} %pad_add_fusion.meta_ref, bf16[8,264,256]{2,1,0:T(8,128)(2,1)S(1)} %all_to_all.38.fresh_ref.recv_ref, bf16[16,256,256]{2,1,0:T(8,128)(2,1)S(1)} %get-tuple-element.6.tiles_ref), custom_call_target="tpu_custom_call" | custom-call | tf_op jit(solution)/shard_map/load_kernel/pallas_call | solution.py:185
  113.1 0.0 copy-start.2
  113.1 0.0 copy-start.4
  113.1 4.3 %all_to_all.39.in_ref = f32[2,32,2176]{2,1,0:T(8,128)S(1)} all-to-all(f32[2,32,2176]{2,1,0:T(8,128)S(1)} %load_kernel.1), channel_id=1, replica_groups=mesh['p'=4,'q'=8,'zh'=2,'x'=4,'core'=2] {'core'}, dimensions={0} | all-to-all | bytes 1114112 | tf_op jit(solution)/shard_map/all_to_all | solution.py:234
  117.4 0.2 encode_kernel.1
  117.6 0.7 convert_element_type.22
  118.3 3.4 %all-to-all-start.6 = ((f16[8,4,2176]{2,1,0:T(4,128)(2,1)}), f16[8,4,2176]{2,1,0:T(4,128)(2,1)S(1)}, u32[]{:S(2)}, u32[]{:S(2)}) async-start(f16[8,4,2176]{2,1,0:T(4,128)(2,1)} %convert_element_type.22), calls=%async_computation.6 | async-start | bytes 278528 | tf_op jit(solution)/shard_map/all_to_all | solution.py:236
  121.7 0.1 pad_add_fusion.1.place_ref
  121.8 1.4 spectra_kernel.1
  123.2 16.6 %all-to-all-done.6 = f16[8,4,2176]{2,1,0:T(4,128)(2,1)S(1)} async-done(((f16[8,4,2176]{2,1,0:T(4,128)(2,1)}), f16[8,4,2176]{2,1,0:T(4,128)(2,1)S(1)}, u32[]{:S(2)}, u32[]{:S(2)}) %all-to-all-start.6) | async-done | bytes 139296 | tf_op jit(solution)/shard_map/all_to_all | solution.py:236
  139.8 1.0 final_kernel.1
  (8 shorter events, 0.1 us)
Async XLA Ops:
  0.6 0.8 copy-start.3
  1.4 20.6 %copy-start.5 = (s32[1,1,16]{2,1,0:T(1,128)S(1)}, s32[1,1,16]{2,1,0:T(1,128)}, u32[]{:S(2)}) copy-start(s32[1,1,16]{2,1,0:T(1,128)} %param.6) | copy-start | bytes 196
  2.0 35.6 %all-to-all-start = ((bf16[8,4,2048]{2,1,0:T(4,128)(2,1)}), bf16[8,4,2048]{2,1,0:T(4,128)(2,1)S(1)}, u32[]{:S(2)}, u32[]{:S(2)}) async-start(bf16[8,4,2048]{2,1,0:T(4,128)(2,1)} %own_kernel.1), calls=%async_computation | async-start | bytes 262144 | tf_op jit(solution)/shard_map/all_to_all | solution.py:201
  19.3 1.6 %copy-start = (bf16[1,1,16,256,256]{4,3,2,1,0:T(8,128)(2,1)S(1)}, bf16[1,1,16,256,256]{4,3,2,1,0:T(8,128)(2,1)}, u32[]{:S(2)}) copy-start(bf16[1,1,16,256,256]{4,3,2,1,0:T(8,128)(2,1)} %param.5) | copy-start | bytes 6291460
  20.9 0.8 copy-start.1
  113.1 8.7 %copy-start.2 = (f32[2,8192]{1,0:T(2,128)S(1)}, f32[2,8192]{1,0:T(2,128)}, u32[]{:S(2)}) copy-start(f32[2,8192]{1,0:T(2,128)} %spec_ref.3) | copy-start | bytes 196612
  113.1 26.7 %copy-start.4 = (f32[4,2048]{1,0:T(4,128)S(1)}, f32[4,2048]{1,0:T(4,128)}, u32[]{:S(2)}) copy-start(f32[4,2048]{1,0:T(4,128)} %loading_ref.3) | copy-start | bytes 98308
  118.3 21.4 %all-to-all-start.6 = ((f16[8,4,2176]{2,1,0:T(4,128)(2,1)}), f16[8,4,2176]{2,1,0:T(4,128)(2,1)S(1)}, u32[]{:S(2)}, u32[]{:S(2)}) async-start(f16[8,4,2176]{2,1,0:T(4,128)(2,1)} %convert_element_type.22), calls=%async_computation.6 | async-start | bytes 278528 | tf_op jit(solution)/shard_map/all_to_all | solution.py:236

commit v5 on v4

--- a/solution.py
+++ b/solution.py
@@ -12,8 +12,8 @@
 NZ, NY, NMASS = 4, 8, 16
 OWN = RANK // NZ
 PER = RANK // NMASS
-TOP_SCALE = 2.0**-10
-GRAM_SCALE = 2.0**-3
+TOP_SCALE = 2.0**-11
+GRAM_SCALE = 2.0**-4
 TOPS = NZ * RANK
 PIXELS = TROWS * TILE
 WIDE = PIXELS + 128

time: 141 us -> 141 us (level)
  no operation moved by 1% of the time
where the time goes in v5:
time: 141 us
  blocking collectives  75.8 us (54%)
  waiting for transfers between devices  32.2 us (23%)
  starting transfers between devices  20 us (14%)
  Pallas kernels  6.83 us (5%)
  local copies, waits for them, and re-layouts  3.19 us (2%)
  between operations  1.42 us (1%)
    all_to_all x1, blocking collectives, local(): part = lax.all_to_all(out.astype(F16), 'q', 0, 0, tiled=True)  21.5 us
    all_to_all x1, blocking collectives, local(): fresh = lax.all_to_all(fresh, 'q', 0, 0, tiled=True)  17.9 us
    all_to_all x1, starting transfers between devices, local(): load = lax.all_to_all(load, ('zh', 'x'), 0, 0, tiled=True)  16.7 us
    all_to_all x1, waiting for transfers between devices, local(): lax.all_to_all(part.astype(F16), ('zh', 'x'), 0, 0, tiled=True).astype(F32)  16.6 us
    all_to_all x1, blocking collectives, local(): part = lax.all_to_all(part.astype(F16), 'p', 0, 0, tiled=True)  16 us
    all_to_all x1, waiting for transfers between devices, local(): load = lax.all_to_all(load, ('zh', 'x'), 0, 0, tiled=True)  15.6 us
    all_to_all x1, blocking collectives, local(): fresh = lax.all_to_all(fresh, 'p', 0, 0, tiled=True)  14.2 us
    pallas_call x9, Pallas kernels, call(): pl.pallas_call(body, out_shape=out, in_specs=specs, out_specs=jax.tree.ma...  6.68 us
  transfers between devices with their start and end apart: 2, of which 2 were waited for; matrix products, arithmetic and copies ran while one was open for 0% of the time, Pallas kernels for 1%

profile of v5, /device:TPU:32, one launch (start us, length us, event | category | flops | bytes accessed | tf_op | source)
XLA Modules:
  0.0 140.8 jit_solution(5099470612796699326)
XLA Ops:
  0.6 0.0 copy-start.3
  0.6 0.7 copy-done.3
  1.4 0.7 own_kernel.1
  2.0 16.7 %all-to-all-start = ((bf16[8,4,2048]{2,1,0:T(4,128)(2,1)}), bf16[8,4,2048]{2,1,0:T(4,128)(2,1)S(1)}, u32[]{:S(2)}, u32[]{:S(2)}) async-start(bf16[8,4,2048]{2,1,0:T(4,128)(2,1)} %own_kernel.1), calls=%async_computation | async-start | bytes 262144 | tf_op jit(solution)/shard_map/all_to_all | solution.py:201
  19.3 0.0 copy-start
  19.4 1.6 %copy-done = bf16[1,1,16,256,256]{4,3,2,1,0:T(8,128)(2,1)S(1)} copy-done((bf16[1,1,16,256,256]{4,3,2,1,0:T(8,128)(2,1)S(1)}, bf16[1,1,16,256,256]{4,3,2,1,0:T(8,128)(2,1)}, u32[]{:S(2)}) %copy-start) | copy-done | bytes 2097176
  20.9 0.8 copy-done.1
  21.8 0.2 fetch_kernel.1
  22.0 0.1 pad_add_fusion.meta_ref
  22.0 15.6 %all-to-all-done = bf16[8,4,2048]{2,1,0:T(4,128)(2,1)S(1)} async-done(((bf16[8,4,2048]{2,1,0:T(4,128)(2,1)}), bf16[8,4,2048]{2,1,0:T(4,128)(2,1)S(1)}, u32[]{:S(2)}, u32[]{:S(2)}) %all-to-all-start) | async-done | bytes 131104 | tf_op jit(solution)/shard_map/all_to_all | solution.py:201
  37.7 2.0 %all-gather = bf16[16,4,2048]{2,1,0:T(4,128)(2,1)S(1)} all-gather(bf16[8,4,2048]{2,1,0:T(4,128)(2,1)S(1)} %all-to-all-done), channel_id=2, replica_groups=mesh['p'=4,'q'=8,'zh'=2,'x'=4,'core'=2] {'core'}, dimensions={0}, use_global_device_ids=true | all-gather | bytes 393216 | tf_op jit(solution)/shard_map/all_gather | solution.py:202
  39.6 1.3 spec_kernel.1
  41.0 0.2 convert_element_type.18
  41.2 21.5 %all_to_all.35 = f16[8,280,256]{2,1,0:T(8,128)(2,1)S(1)} all-to-all(f16[8,280,256]{2,1,0:T(8,128)(2,1)S(1)} %convert_element_type.18), channel_id=1, replica_groups=mesh['p'=4,'q'=8,'zh'=2,'x'=4,'core'=2] {'q'}, dimensions={0} | all-to-all | bytes 2293760 | tf_op jit(solution)/shard_map/all_to_all | solution.py:219
  62.7 0.2 convert_element_type.19.in_ref
  62.8 0.1 middle_kernel.1
  63.0 16.0 %all_to_all.36 = f16[4,96,256]{2,1,0:T(8,128)(2,1)S(1)} all-to-all(f16[4,96,256]{2,1,0:T(8,128)(2,1)S(1)} %convert_element_type.20), channel_id=1, replica_groups=mesh['p'=4,'q'=8,'zh'=2,'x'=4,'core'=2] {'p'}, dimensions={0} | all-to-all | bytes 393216 | tf_op jit(solution)/shard_map/all_to_all | solution.py:221
  79.0 0.3 update_kernel.1
  79.3 14.2 %all_to_all.37.in_ref = bf16[4,80,256]{2,1,0:T(8,128)(2,1)S(1)} all-to-all(bf16[4,80,256]{2,1,0:T(8,128)(2,1)S(1)} %update_kernel.1), channel_id=1, replica_groups=mesh['p'=4,'q'=8,'zh'=2,'x'=4,'core'=2] {'p'}, dimensions={0} | all-to-all | bytes 327680 | tf_op jit(solution)/shard_map/all_to_all | solution.py:224
  93.5 0.1 spread_kernel.1
  93.6 17.9 %all_to_all.38.fresh_ref.recv_ref = bf16[8,264,256]{2,1,0:T(8,128)(2,1)S(1)} all-to-all(bf16[8,264,256]{2,1,0:T(8,128)(2,1)S(1)} %spread_kernel.1), channel_id=1, replica_groups=mesh['p'=4,'q'=8,'zh'=2,'x'=4,'core'=2] {'q'}, dimensions={0} | all-to-all | bytes 2162688 | tf_op jit(solution)/shard_map/all_to_all | solution.py:226
  111.5 1.6 %load_kernel.1 = f32[2,32,2176]{2,1,0:T(8,128)S(1)} custom-call(s32[17]{0:T(128)S(1)} %pad_add_fusion.meta_ref, bf16[8,264,256]{2,1,0:T(8,128)(2,1)S(1)} %all_to_all.38.fresh_ref.recv_ref, bf16[16,256,256]{2,1,0:T(8,128)(2,1)S(1)} %get-tuple-element.6.tiles_ref), custom_call_target="tpu_custom_call" | custom-call | tf_op jit(solution)/shard_map/load_kernel/pallas_call | solution.py:185
  113.1 0.0 copy-start.2
  113.1 0.0 copy-start.4
  113.1 4.3 %all_to_all.39.in_ref = f32[2,32,2176]{2,1,0:T(8,128)S(1)} all-to-all(f32[2,32,2176]{2,1,0:T(8,128)S(1)} %load_kernel.1), channel_id=1, replica_groups=mesh['p'=4,'q'=8,'zh'=2,'x'=4,'core'=2] {'core'}, dimensions={0} | all-to-all | bytes 1114112 | tf_op jit(solution)/shard_map/all_to_all | solution.py:234
  117.4 0.2 encode_kernel.1
  117.6 0.7 convert_element_type.22
  118.3 3.4 %all-to-all-start.6 = ((f16[8,4,2176]{2,1,0:T(4,128)(2,1)}), f16[8,4,2176]{2,1,0:T(4,128)(2,1)S(1)}, u32[]{:S(2)}, u32[]{:S(2)}) async-start(f16[8,4,2176]{2,1,0:T(4,128)(2,1)} %convert_element_type.22), calls=%async_computation.6 | async-start | bytes 278528 | tf_op jit(solution)/shard_map/all_to_all | solution.py:236
  121.7 0.1 pad_add_fusion.1.place_ref
  121.8 1.4 spectra_kernel.1
  123.2 16.6 %all-to-all-done.6 = f16[8,4,2176]{2,1,0:T(4,128)(2,1)S(1)} async-done(((f16[8,4,2176]{2,1,0:T(4,128)(2,1)}), f16[8,4,2176]{2,1,0:T(4,128)(2,1)S(1)}, u32[]{:S(2)}, u32[]{:S(2)}) %all-to-all-start.6) | async-done | bytes 139296 | tf_op jit(solution)/shard_map/all_to_all | solution.py:236
  139.8 1.0 final_kernel.1
  (8 shorter events, 0.1 us)
Async XLA Ops:
  0.6 0.8 copy-start.3
  1.4 20.6 %copy-start.5 = (s32[1,1,16]{2,1,0:T(1,128)S(1)}, s32[1,1,16]{2,1,0:T(1,128)}, u32[]{:S(2)}) copy-start(s32[1,1,16]{2,1,0:T(1,128)} %param.6) | copy-start | bytes 196
  2.0 35.6 %all-to-all-start = ((bf16[8,4,2048]{2,1,0:T(4,128)(2,1)}), bf16[8,4,2048]{2,1,0:T(4,128)(2,1)S(1)}, u32[]{:S(2)}, u32[]{:S(2)}) async-start(bf16[8,4,2048]{2,1,0:T(4,128)(2,1)} %own_kernel.1), calls=%async_computation | async-start | bytes 262144 | tf_op jit(solution)/shard_map/all_to_all | solution.py:201
  19.3 1.6 %copy-start = (bf16[1,1,16,256,256]{4,3,2,1,0:T(8,128)(2,1)S(1)}, bf16[1,1,16,256,256]{4,3,2,1,0:T(8,128)(2,1)}, u32[]{:S(2)}) copy-start(bf16[1,1,16,256,256]{4,3,2,1,0:T(8,128)(2,1)} %param.5) | copy-start | bytes 6291460
  20.9 0.8 copy-start.1
  113.1 8.7 %copy-start.2 = (f32[2,8192]{1,0:T(2,128)S(1)}, f32[2,8192]{1,0:T(2,128)}, u32[]{:S(2)}) copy-start(f32[2,8192]{1,0:T(2,128)} %spec_ref.3) | copy-start | bytes 196612
  113.1 26.7 %copy-start.4 = (f32[4,2048]{1,0:T(4,128)S(1)}, f32[4,2048]{1,0:T(4,128)}, u32[]{:S(2)}) copy-start(f32[4,2048]{1,0:T(4,128)} %loading_ref.3) | copy-start | bytes 98308
  118.3 21.4 %all-to-all-start.6 = ((f16[8,4,2176]{2,1,0:T(4,128)(2,1)}), f16[8,4,2176]{2,1,0:T(4,128)(2,1)S(1)}, u32[]{:S(2)}, u32[]{:S(2)}) async-start(f16[8,4,2176]{2,1,0:T(4,128)(2,1)} %convert_element_type.22), calls=%async_computation.6 | async-start | bytes 278528 | tf_op jit(solution)/shard_map/all_to_all | solution.py:236

commit v6 on v5

--- a/solution.py
+++ b/solution.py
@@ -157,7 +157,13 @@
         tail = part_ref[m, :, pl.ds(PIXELS, 128)]
         top = top + part_ref[m, :, pl.ds(0, PIXELS)] * jnp.exp2(tail[:, RANK : RANK + 1])
         gram = gram + tail[:, :RANK] * jnp.exp2(tail[:, RANK + 1 : RANK + 2])
-    bottom = jnp.dot(gram, half_ref[...].astype(F32), precision=lax.Precision.HIGHEST, preferred_element_type=F32)
+    high = gram.astype(BF16)
+    rest = gram - high.astype(F32)
+    middle = rest.astype(BF16)
+    low = (rest - middle.astype(F32)).astype(BF16)
+    parts = jnp.concatenate([x.astype(F32) for x in (high, middle, low, low)], axis=0).astype(BF16)
+    sums = jnp.dot(parts, half_ref[...], preferred_element_type=F32)
+    bottom = (sums[2 * PER : 3 * PER] + sums[PER : 2 * PER]) + sums[:PER]
     out_ref[...] = loading_ref[...] * top / bottom
 
 

time: 141 us -> 141 us (level)
  no operation moved by 1% of the time
where the time goes in v6:
time: 141 us
  blocking collectives  75.8 us (54%)
  waiting for transfers between devices  32.2 us (23%)
  starting transfers between devices  20 us (14%)
  Pallas kernels  6.68 us (5%)
  local copies, waits for them, and re-layouts  3.19 us (2%)
  between operations  1.42 us (1%)
    all_to_all x1, blocking collectives, local(): part = lax.all_to_all(out.astype(F16), 'q', 0, 0, tiled=True)  21.5 us
    all_to_all x1, blocking collectives, local(): fresh = lax.all_to_all(fresh, 'q', 0, 0, tiled=True)  17.9 us
    all_to_all x1, starting transfers between devices, local(): load = lax.all_to_all(load, ('zh', 'x'), 0, 0, tiled=True)  16.7 us
    all_to_all x1, waiting for transfers between devices, local(): lax.all_to_all(part.astype(F16), ('zh', 'x'), 0, 0, tiled=True).astype(F32)  16.6 us
    all_to_all x1, blocking collectives, local(): part = lax.all_to_all(part.astype(F16), 'p', 0, 0, tiled=True)  16 us
    all_to_all x1, waiting for transfers between devices, local(): load = lax.all_to_all(load, ('zh', 'x'), 0, 0, tiled=True)  15.6 us
    all_to_all x1, blocking collectives, local(): fresh = lax.all_to_all(fresh, 'p', 0, 0, tiled=True)  14.2 us
    pallas_call x9, Pallas kernels, call(): pl.pallas_call(body, out_shape=out, in_specs=specs, out_specs=jax.tree.ma...  6.52 us
  transfers between devices with their start and end apart: 2, of which 2 were waited for; matrix products, arithmetic and copies ran while one was open for 0% of the time, Pallas kernels for 1%

profile of v6, /device:TPU:32, one launch (start us, length us, event | category | flops | bytes accessed | tf_op | source)
XLA Modules:
  0.0 140.7 jit_solution(11436937698882735028)
XLA Ops:
  0.6 0.0 copy-start.3
  0.6 0.7 copy-done.3
  1.4 0.7 own_kernel.1
  2.0 16.7 %all-to-all-start = ((bf16[8,4,2048]{2,1,0:T(4,128)(2,1)}), bf16[8,4,2048]{2,1,0:T(4,128)(2,1)S(1)}, u32[]{:S(2)}, u32[]{:S(2)}) async-start(bf16[8,4,2048]{2,1,0:T(4,128)(2,1)} %own_kernel.1), calls=%async_computation | async-start | bytes 262144 | tf_op jit(solution)/shard_map/all_to_all | solution.py:207
  19.3 0.0 copy-start
  19.4 1.6 %copy-done = bf16[1,1,16,256,256]{4,3,2,1,0:T(8,128)(2,1)S(1)} copy-done((bf16[1,1,16,256,256]{4,3,2,1,0:T(8,128)(2,1)S(1)}, bf16[1,1,16,256,256]{4,3,2,1,0:T(8,128)(2,1)}, u32[]{:S(2)}) %copy-start) | copy-done | bytes 2097176
  20.9 0.8 copy-done.1
  21.8 0.2 fetch_kernel.1
  22.0 0.1 pad_add_fusion.meta_ref
  22.0 15.6 %all-to-all-done = bf16[8,4,2048]{2,1,0:T(4,128)(2,1)S(1)} async-done(((bf16[8,4,2048]{2,1,0:T(4,128)(2,1)}), bf16[8,4,2048]{2,1,0:T(4,128)(2,1)S(1)}, u32[]{:S(2)}, u32[]{:S(2)}) %all-to-all-start) | async-done | bytes 131104 | tf_op jit(solution)/shard_map/all_to_all | solution.py:207
  37.7 2.0 %all-gather = bf16[16,4,2048]{2,1,0:T(4,128)(2,1)S(1)} all-gather(bf16[8,4,2048]{2,1,0:T(4,128)(2,1)S(1)} %all-to-all-done), channel_id=2, replica_groups=mesh['p'=4,'q'=8,'zh'=2,'x'=4,'core'=2] {'core'}, dimensions={0}, use_global_device_ids=true | all-gather | bytes 393216 | tf_op jit(solution)/shard_map/all_gather | solution.py:208
  39.6 1.3 spec_kernel.1
  41.0 0.2 convert_element_type.18
  41.2 21.5 %all_to_all.35 = f16[8,280,256]{2,1,0:T(8,128)(2,1)S(1)} all-to-all(f16[8,280,256]{2,1,0:T(8,128)(2,1)S(1)} %convert_element_type.18), channel_id=1, replica_groups=mesh['p'=4,'q'=8,'zh'=2,'x'=4,'core'=2] {'q'}, dimensions={0} | all-to-all | bytes 2293760 | tf_op jit(solution)/shard_map/all_to_all | solution.py:225
  62.7 0.2 convert_element_type.19.in_ref
  62.8 0.1 middle_kernel.1
  63.0 16.0 %all_to_all.36 = f16[4,96,256]{2,1,0:T(8,128)(2,1)S(1)} all-to-all(f16[4,96,256]{2,1,0:T(8,128)(2,1)S(1)} %convert_element_type.20), channel_id=1, replica_groups=mesh['p'=4,'q'=8,'zh'=2,'x'=4,'core'=2] {'p'}, dimensions={0} | all-to-all | bytes 393216 | tf_op jit(solution)/shard_map/all_to_all | solution.py:227
  79.0 0.3 update_kernel.1
  79.3 14.2 %all_to_all.37.in_ref = bf16[4,80,256]{2,1,0:T(8,128)(2,1)S(1)} all-to-all(bf16[4,80,256]{2,1,0:T(8,128)(2,1)S(1)} %update_kernel.1), channel_id=1, replica_groups=mesh['p'=4,'q'=8,'zh'=2,'x'=4,'core'=2] {'p'}, dimensions={0} | all-to-all | bytes 327680 | tf_op jit(solution)/shard_map/all_to_all | solution.py:230
  93.5 0.1 spread_kernel.1
  93.6 17.9 %all_to_all.38.fresh_ref.recv_ref = bf16[8,264,256]{2,1,0:T(8,128)(2,1)S(1)} all-to-all(bf16[8,264,256]{2,1,0:T(8,128)(2,1)S(1)} %spread_kernel.1), channel_id=1, replica_groups=mesh['p'=4,'q'=8,'zh'=2,'x'=4,'core'=2] {'q'}, dimensions={0} | all-to-all | bytes 2162688 | tf_op jit(solution)/shard_map/all_to_all | solution.py:232
  111.5 1.6 %load_kernel.1 = f32[2,32,2176]{2,1,0:T(8,128)S(1)} custom-call(s32[17]{0:T(128)S(1)} %pad_add_fusion.meta_ref, bf16[8,264,256]{2,1,0:T(8,128)(2,1)S(1)} %all_to_all.38.fresh_ref.recv_ref, bf16[16,256,256]{2,1,0:T(8,128)(2,1)S(1)} %get-tuple-element.6.tiles_ref), custom_call_target="tpu_custom_call" | custom-call | tf_op jit(solution)/shard_map/load_kernel/pallas_call | solution.py:191
  113.1 0.0 copy-start.2
  113.1 0.0 copy-start.4
  113.1 4.3 %all_to_all.39.in_ref = f32[2,32,2176]{2,1,0:T(8,128)S(1)} all-to-all(f32[2,32,2176]{2,1,0:T(8,128)S(1)} %load_kernel.1), channel_id=1, replica_groups=mesh['p'=4,'q'=8,'zh'=2,'x'=4,'core'=2] {'core'}, dimensions={0} | all-to-all | bytes 1114112 | tf_op jit(solution)/shard_map/all_to_all | solution.py:240
  117.4 0.2 encode_kernel.1
  117.6 0.7 convert_element_type.22
  118.3 3.4 %all-to-all-start.6 = ((f16[8,4,2176]{2,1,0:T(4,128)(2,1)}), f16[8,4,2176]{2,1,0:T(4,128)(2,1)S(1)}, u32[]{:S(2)}, u32[]{:S(2)}) async-start(f16[8,4,2176]{2,1,0:T(4,128)(2,1)} %convert_element_type.22), calls=%async_computation.6 | async-start | bytes 278528 | tf_op jit(solution)/shard_map/all_to_all | solution.py:242
  121.7 0.1 pad_add_fusion.1.place_ref
  121.8 1.4 spectra_kernel.1
  123.2 16.6 %all-to-all-done.6 = f16[8,4,2176]{2,1,0:T(4,128)(2,1)S(1)} async-done(((f16[8,4,2176]{2,1,0:T(4,128)(2,1)}), f16[8,4,2176]{2,1,0:T(4,128)(2,1)S(1)}, u32[]{:S(2)}, u32[]{:S(2)}) %all-to-all-start.6) | async-done | bytes 139296 | tf_op jit(solution)/shard_map/all_to_all | solution.py:242
  139.8 0.9 final_kernel.1
  (8 shorter events, 0.1 us)
Async XLA Ops:
  0.6 0.8 copy-start.3
  1.4 20.6 %copy-start.5 = (s32[1,1,16]{2,1,0:T(1,128)S(1)}, s32[1,1,16]{2,1,0:T(1,128)}, u32[]{:S(2)}) copy-start(s32[1,1,16]{2,1,0:T(1,128)} %param.6) | copy-start | bytes 196
  2.0 35.6 %all-to-all-start = ((bf16[8,4,2048]{2,1,0:T(4,128)(2,1)}), bf16[8,4,2048]{2,1,0:T(4,128)(2,1)S(1)}, u32[]{:S(2)}, u32[]{:S(2)}) async-start(bf16[8,4,2048]{2,1,0:T(4,128)(2,1)} %own_kernel.1), calls=%async_computation | async-start | bytes 262144 | tf_op jit(solution)/shard_map/all_to_all | solution.py:207
  19.3 1.6 %copy-start = (bf16[1,1,16,256,256]{4,3,2,1,0:T(8,128)(2,1)S(1)}, bf16[1,1,16,256,256]{4,3,2,1,0:T(8,128)(2,1)}, u32[]{:S(2)}) copy-start(bf16[1,1,16,256,256]{4,3,2,1,0:T(8,128)(2,1)} %param.5) | copy-start | bytes 6291460
  20.9 0.8 copy-start.1
  113.1 8.7 %copy-start.2 = (f32[2,8192]{1,0:T(2,128)S(1)}, f32[2,8192]{1,0:T(2,128)}, u32[]{:S(2)}) copy-start(f32[2,8192]{1,0:T(2,128)} %spec_ref.3) | copy-start | bytes 196612
  113.1 26.7 %copy-start.4 = (f32[4,2048]{1,0:T(4,128)S(1)}, f32[4,2048]{1,0:T(4,128)}, u32[]{:S(2)}) copy-start(f32[4,2048]{1,0:T(4,128)} %loading_ref.3) | copy-start | bytes 98308
  118.3 21.4 %all-to-all-start.6 = ((f16[8,4,2176]{2,1,0:T(4,128)(2,1)}), f16[8,4,2176]{2,1,0:T(4,128)(2,1)S(1)}, u32[]{:S(2)}, u32[]{:S(2)}) async-start(f16[8,4,2176]{2,1,0:T(4,128)(2,1)} %convert_element_type.22), calls=%async_computation.6 | async-start | bytes 278528 | tf_op jit(solution)/shard_map/all_to_all | solution.py:242
